TPU v7x, 32 devices: a whole 2x2x4 slice. The times are simulated.
32 devices in a mesh: terms: 8 (over y, x, core), rows: 4 (over z).
Axes of the slice: x: 2, y: 2, z: 4, core: 2. Of those that a mesh axis runs over, the one named last changes fastest.
Arguments:
- amplitudes: float32 [768, 768], P('rows'), may hold values from -6 to 6
- left_terms: float32 [8, 768, 768], P('terms', 'rows'), may hold values from -0.078125 to 0.078125
- right_terms: float32 [8, 768, 768], P('terms'), may hold values from -0.21875 to 0.21875
- source_list: int32 [8, 4], replicated, may hold values from 0 to 7, as said below
- list_count: int32 [8], replicated, may hold values from 1 to 4
- weight_index: int32 [8, 4], replicated, may hold values from 0 to 7
- weight_table: float32 [8], replicated, may hold values from -4 to 4
Outputs:
- isometry: float32 [768, 768], P('rows')
- new_environment: float32 [8, 768, 768], P('terms', 'rows')
Inputs may be any that keep to these rules, and one draw needn't show every extreme that they name: `source_list`: every block id appears in column 0 exactly once.
All inputs are finite; a program needn't handle non-finite values.
Results may differ from a plain program's by a relative error of at most 0.00016.
Values sent between devices are 32-bit elements; how exact they have to be, the bound alone decides.
No kernel may reach another device: no remote copies, remote signals or barrier semaphores. Data moves between devices by JAX's collectives and lax.ppermute only.
A program may use at most 64 MiB of HBM per device.

v0:
```python
import functools
import math

import jax
import jax.numpy as jnp
from jax import lax
from jax.experimental import pallas as pl
from jax.experimental.pallas import tpu as pltpu
from jax.sharding import PartitionSpec as P


SWEEPS = 3

HIGH = lax.Precision.HIGHEST
COEF_ONE = 3.4445
COEF_TWO = -4.775
COEF_THREE = 2.0315
STEP = 0.3


VMEM = pl.BlockSpec(memory_space=pltpu.VMEM)
SMEM = pl.BlockSpec(memory_space=pltpu.SMEM)
MIB = 1 << 20
BF16 = jnp.bfloat16
F32 = jnp.float32


def halves(value):
    high = value.astype(BF16)
    low = (value - high.astype(F32)).astype(BF16)
    return high, low


def product(left, right, over=(1, 0)):
    dims = (((over[0],), (over[1],)), ((), ()))
    dot = functools.partial(lax.dot_general, dimension_numbers=dims, preferred_element_type=F32)
    return dot(left[0], right[0]) + (dot(left[0], right[1]) + dot(left[1], right[0]))


def shape(dims, dtype=F32):
    return jax.ShapeDtypeStruct(dims, dtype)


class Places:
    def __init__(self, terms, rows, slab):
        self.terms, self.rows, self.slab = terms, rows, slab
        self.cores = 2
        self.chips = terms // self.cores
        self.piece = slab // terms
        self.half = slab // self.cores

    def here(self):
        term = lax.axis_index("terms")
        return term // self.cores, term % self.cores, lax.axis_index("rows")

    def swap(self, value, chip=0, core=0, row=0):
        pairs = []
        for term in range(self.terms):
            for line in range(self.rows):
                other = term ^ (chip * self.cores + core)
                pairs.append((term * self.rows + line, other * self.rows + (line ^ row)))
        return lax.ppermute(value, ("terms", "rows"), pairs)


def prepare(places, left, right):
    piece, half = places.piece, places.half

    def kernel(left_ref, right_ref, lh_ref, ll_ref, rh_ref, rl_ref, ordered):
        chip, core, _ = places.here()
        for side in range(places.cores):
            for slot in range(places.chips):
                source = (core ^ side) * half + (chip ^ slot) * piece
                source = pl.multiple_of(source, 8)
                ordered[pl.ds(side * half + slot * piece, piece), :] = left_ref[pl.ds(source, piece), :]
        lh_ref[...], ll_ref[...] = halves(ordered[...])
        rh_ref[...], rl_ref[...] = halves(right_ref[...])

    return pl.pallas_call(
        kernel,
        out_shape=(shape(left.shape, BF16),) * 2 + (shape(right.shape, BF16),) * 2,
        in_specs=[VMEM, VMEM],
        out_specs=(VMEM,) * 4,
        scratch_shapes=[pltpu.VMEM(left.shape, F32)],
        compiler_params=pltpu.CompilerParams(vmem_limit_bytes=12 * MIB),
        name="prepare",
    )(left, right)


def assemble(places, layout, parts, store):
    chip, core, line = places.here()
    for (chip_slot, core_slot, row_slots, rows_each), part in zip(layout, parts):
        for index, row_slot in enumerate(row_slots):
            start = (line ^ row_slot) * places.slab
            if rows_each != places.slab:
                start = start + (core ^ core_slot) * places.half + (chip ^ chip_slot) * places.piece
            store(pl.multiple_of(start, 8), rows_each, part[pl.ds(index * rows_each, rows_each), :])


def put_in(whole):
    def store(start, height, value):
        whole[pl.ds(start, height), :] = value

    return store


def apply_terms(places, layout, parts, prepared):
    width = parts[0].shape[1]
    half = places.half

    def kernel(*refs):
        count = len(parts)
        lh_ref, ll_ref, rh_ref, rl_ref, keep_ref, send_ref, whole = refs[count:]
        assemble(places, layout, refs[:count], put_in(whole))
        mapped = product((lh_ref[...], ll_ref[...]), halves(whole[...]))
        total = product(halves(mapped), (rh_ref[...], rl_ref[...]))
        keep_ref[...] = total[:half]
        send_ref[...] = total[half:]

    return pl.pallas_call(
        kernel,
        out_shape=(shape((half, width)),) * 2,
        in_specs=[VMEM] * (len(parts) + 4),
        out_specs=(VMEM, VMEM),
        scratch_shapes=[pltpu.VMEM((width, width), F32)],
        compiler_params=pltpu.CompilerParams(vmem_limit_bytes=16 * MIB),
        name="apply",
    )(*parts, *prepared)


def add_pieces(places, keep, received):
    piece = places.piece
    width = keep.shape[1]

    def kernel(keep_ref, received_ref, *outs):
        for slot, out in enumerate(outs):
            rows = pl.ds(slot * piece, piece)
            out[...] = keep_ref[rows, :] + received_ref[rows, :]

    return pl.pallas_call(
        kernel,
        out_shape=(shape((piece, width)),) * places.chips,
        in_specs=[VMEM, VMEM],
        out_specs=(VMEM,) * places.chips,
        compiler_params=pltpu.CompilerParams(vmem_limit_bytes=2 * MIB),
        name="add_pieces",
    )(keep, received)


def step_piece(base, pieces):
    def kernel(base_ref, *refs):
        total = refs[0][...]
        for ref in refs[1:-1]:
            total = total + ref[...]
        refs[-1][...] = base_ref[...] - STEP * total

    return pl.pallas_call(
        kernel,
        out_shape=shape(base.shape),
        in_specs=[VMEM] * (1 + len(pieces)),
        out_specs=VMEM,
        compiler_params=pltpu.CompilerParams(vmem_limit_bytes=2 * MIB),
        name="step_piece",
    )(base, *pieces)


def stack(parts):
    width = parts[0].shape[1]
    heights = [part.shape[0] for part in parts]

    def kernel(*refs):
        out = refs[-1]
        start = 0
        for ref, height in zip(refs[:-1], heights):
            out[pl.ds(start, height), :] = ref[...]
            start += height

    return pl.pallas_call(
        kernel,
        out_shape=shape((sum(heights), width)),
        in_specs=[VMEM] * len(parts),
        out_specs=VMEM,
        compiler_params=pltpu.CompilerParams(vmem_limit_bytes=2 * MIB),
        name="stack",
    )(*parts)


def spread(places, piece, with_own=True, ready=()):
    slots = [0] if with_own else []
    lines = [piece] if with_own else []
    for slot in reversed(range(1, places.rows)):
        slots.append(slot)
        lines.append(places.swap(piece, row=slot))
    mine = stack(lines)
    if ready:
        mine, *ready = lax.optimization_barrier((mine, *ready))
    chips = [mine] + [places.swap(mine, chip=slot) for slot in range(1, places.chips)]
    layout, parts = [], []
    for core_slot in range(places.cores):
        for slot, part in enumerate(chips):
            layout.append((slot, core_slot, slots, places.piece))
            parts.append(places.swap(part, core=core_slot) if core_slot else part)
    return layout, parts, ready


def reduced(places, keep, send):
    received = places.swap(send, core=1)
    own, *others = add_pieces(places, keep, received)
    return [own] + [places.swap(part, chip=slot + 1) for slot, part in enumerate(others)]


def orthogonal(places, layout, parts):
    width = parts[0].shape[1]
    slab = places.slab
    tile = 256 if width % 256 == 0 else width
    blocks = width // tile

    def kernel(*refs):
        count = len(parts)
        slab_ref, high, low, iterate, gram, poly, gram_high, gram_low, poly_high, poly_low = refs[count:]
        assemble(places, layout, refs[:count], put_in(gram))
        values = gram[...].T
        values = values * (1.0 / jnp.sqrt(jnp.sum(values * values)))
        iterate[...] = values
        high[...], low[...] = halves(values)

        def symmetric(out, left, over, finish):
            for i in range(blocks):
                rows = pl.ds(i * tile, tile)
                rest = pl.ds(i * tile, width - i * tile)
                if over == (1, 1):
                    right = (left[0][rest, :], left[1][rest, :])
                else:
                    right = (left[0][:, rest], left[1][:, rest])
                strip = finish(product((left[0][rows, :], left[1][rows, :]), right, over), rows, rest)
                out[rows, rest] = strip
                for j in range(i + 1, blocks):
                    out[pl.ds(j * tile, tile), rows] = strip[:, (j - i) * tile : (j - i + 1) * tile].T

        for repeat in range(SWEEPS):
            symmetric(gram, (high, low), (1, 1), lambda value, rows, rest: value)
            gram_high[...], gram_low[...] = halves(gram[...])
            symmetric(
                poly,
                (gram_high, gram_low),
                (1, 0),
                lambda value, rows, rest: COEF_TWO * gram[rows, rest] + COEF_THREE * value,
            )
            poly_high[...], poly_low[...] = halves(poly[...])
            right = (high[...], low[...])
            scale = math.sqrt(width) if repeat == SWEEPS - 1 else 1.0
            for i in range(blocks):
                rows = pl.ds(i * tile, tile)
                moved = product((poly_high[rows, :], poly_low[rows, :]), right)
                iterate[rows, :] = scale * (COEF_ONE * iterate[rows, :] + moved)
            high[...], low[...] = halves(iterate[...])
        gram[...] = iterate[...].T
        line = lax.axis_index("rows")
        slab_ref[...] = gram[pl.ds(pl.multiple_of(line * slab, 8), slab), :]

    square = (width, width)
    return pl.pallas_call(
        kernel,
        out_shape=(shape((slab, width)),) + (shape(square, BF16),) * 2,
        in_specs=[VMEM] * len(parts),
        out_specs=(VMEM,) * 3,
        scratch_shapes=[pltpu.VMEM(square, F32)] * 3 + [pltpu.VMEM(square, BF16)] * 4,
        compiler_params=pltpu.CompilerParams(vmem_limit_bytes=40 * MIB),
        name="orthogonal",
    )(*parts)


def environment(places, layout, parts, high, low):
    width = high.shape[0]
    slab = places.slab

    def kernel(*refs):
        count = len(parts)
        high_ref, low_ref, out_ref, block_high, block_low = refs[count:]

        def store(start, height, value):
            block_high[pl.ds(start, height), :], block_low[pl.ds(start, height), :] = halves(value)

        assemble(places, layout, refs[:count], store)
        rows = pl.ds(pl.multiple_of(lax.axis_index("rows") * slab, 16), slab)
        rotated = product((high_ref[rows, :], low_ref[rows, :]), (block_high[...], block_low[...]))
        out_ref[...] = product(halves(rotated), (high_ref[...], low_ref[...]), (1, 1))

    return pl.pallas_call(
        kernel,
        out_shape=shape((slab, width)),
        in_specs=[VMEM] * (len(parts) + 2),
        out_specs=VMEM,
        scratch_shapes=[pltpu.VMEM((width, width), BF16)] * 2,
        compiler_params=pltpu.CompilerParams(vmem_limit_bytes=16 * MIB),
        name="environment",
    )(*parts, high, low)


def combine_pieces(pieces, source_list, list_count, weight_index, weight_table):
    fan = source_list.shape[1]

    def kernel(source_ref, count_ref, index_ref, table_ref, pieces_ref, out_ref):
        for j in range(source_list.shape[0]):
            total = None
            for c in range(fan):
                weight = jnp.where(c < count_ref[j], table_ref[index_ref[j, c]], 0.0)
                term = weight * pieces_ref[source_ref[j, c]]
                total = term if total is None else total + term
            out_ref[j] = total

    return pl.pallas_call(
        kernel,
        out_shape=shape((source_list.shape[0],) + pieces.shape[1:]),
        in_specs=[SMEM] * 4 + [VMEM],
        out_specs=VMEM,
        compiler_params=pltpu.CompilerParams(vmem_limit_bytes=4 * MIB),
        name="combine",
    )(source_list, list_count, weight_index, weight_table, pieces)


def combined_slab(left, source_list, list_count, weight_index, weight_table):
    rows, width = left.shape
    owners = lax.axis_size("terms")
    if rows % (8 * owners) == 0:
        run = (rows // owners, width)
    else:
        run = (1, rows * width // owners)
    pieces = lax.all_to_all(left.reshape((owners,) + run), "terms", 0, 0, tiled=True)
    mixed = combine_pieces(pieces, source_list, list_count, weight_index, weight_table)
    return mixed, lax.all_to_all(mixed, "terms", 0, 0, tiled=True).reshape(rows, width)


def body(amplitudes, left_terms, right_terms, source_list, list_count, weight_index, weight_table):
    left, right = left_terms[0], right_terms[0]
    slab, _ = left.shape
    terms, rows = lax.axis_size("terms"), lax.axis_size("rows")
    places = Places(terms, rows, slab)

    _, combined = combined_slab(left, source_list, list_count, weight_index, weight_table)
    chip, core, line = places.here()
    every = list(range(rows))
    slabs = [(0, 0, [slot], slab) for slot in every]
    if swappable(terms, rows, slab):
        prepared = prepare(places, left, right)
        start = core * places.half + chip * places.piece
        base = lax.dynamic_slice_in_dim(amplitudes, start, places.piece, 0)
        layout, parts, prepared = spread(places, base, with_own=False, ready=prepared)
        layout, parts = [slabs[0]] + layout, [amplitudes] + parts
        for _ in range(2):
            keep, send = apply_terms(places, layout, parts, prepared)
            base = step_piece(base, reduced(places, keep, send))
            layout, parts, _ = spread(places, base)
        blocks = [combined]
        for slot in every[1:]:
            blocks.append(places.swap(combined, row=slot))
    else:
        matrix = amplitudes
        for _ in range(2):
            full = lax.all_gather(matrix, "rows", axis=0, tiled=True)
            mapped = jnp.dot(left, full, precision=HIGH)
            summed = lax.psum(jnp.dot(mapped, right, precision=HIGH), "terms")
            matrix = matrix - STEP * summed
        full = lax.all_gather(matrix, "rows", axis=0, tiled=True)
        layout = slabs
        parts = [lax.dynamic_slice_in_dim(full, (line ^ slot) * slab, slab, 0) for slot in every]
        full = lax.all_gather(combined, "rows", axis=0, tiled=True)
        blocks = [lax.dynamic_slice_in_dim(full, (line ^ slot) * slab, slab, 0) for slot in every]
    isometry, high, low = orthogonal(places, layout, parts)
    new_environment = environment(places, slabs, blocks, high, low)
    return (isometry, new_environment[None])


def swappable(terms, rows, slab):
    return terms <= 8 and terms & (terms - 1) == 0 and rows & (rows - 1) == 0 and slab % (8 * terms) == 0


def solution(mesh):
    placed = (P("rows", None), P("terms", "rows", None), P("terms", None, None), P(), P(), P(), P())

    return jax.shard_map(
        body,
        mesh=mesh,
        in_specs=placed,
        out_specs=(P("rows", None), P("terms", "rows", None)),
        check_vma=False,
    )
```

profile of v0, /device:TPU:8, one launch (start us, length us, event | category | flops | bytes accessed | tf_op | source)
XLA Modules:
  0.0 171.8 jit_solution(12316542593295148406)
XLA Ops:
  14.4 4.8 %collective-permute-done.3.refs_2_ = f32[72,768]{1,0:T(8,128)S(1)} collective-permute-done((f32[72,768]{1,0:T(8,128)S(1)}, f32[72,768]{1,0:T(8,128)S(1)}, u32[]{:S(2)}, u32[]{:S(2)}) %collective-permute-start.3) | collective-permute-done | bytes 221216 | tf_op jit(solution)/shard_map/ppermute | solution.py:62
  19.2 3.7 %collective-permute-done.4.refs_3_ = f32[72,768]{1,0:T(8,128)S(1)} collective-permute-done((f32[72,768]{1,0:T(8,128)S(1)}, f32[72,768]{1,0:T(8,128)S(1)}, u32[]{:S(2)}, u32[]{:S(2)}) %collective-permute-start.4) | collective-permute-done | bytes 221216 | tf_op jit(solution)/shard_map/ppermute | solution.py:62
  24.7 3.0 %apply.2 = (f32[96,768]{1,0:T(8,128)S(1)}, f32[96,768]{1,0:T(8,128)S(1)}) custom-call(f32[192,768]{1,0:T(8,128)S(1)} %copy-done.3, f32[72,768]{1,0:T(8,128)S(1)} %stack.3.refs_1_, f32[72,768]{1,0:T(8,128)S(1)} %collective-permute-done.3.refs_2_, f32[72,768]{1,0:T(8,128)S(1)} %collective-permute-done.4.refs_3_, f32[72,768]{1,0:T(8,128)S(1)} %collective-permute-done.5.refs_4_, ...), custom_call_target="tpu_custom_call" | custom-call | tf_op jit(solution)/shard_map/apply/pallas_call | solution.py:119
  34.8 2.0 %collective-permute-done.13.refs_3_ = f32[24,768]{1,0:T(8,128)S(1)} collective-permute-done((f32[24,768]{1,0:T(8,128)S(1)}, f32[24,768]{1,0:T(8,128)S(1)}, u32[]{:S(2)}, u32[]{:S(2)}) %collective-permute-start.13) | collective-permute-done | bytes 73760 | tf_op jit(solution)/shard_map/ppermute | solution.py:62
  37.2 3.9 %collective-permute-start.15 = (f32[24,768]{1,0:T(8,128)S(1)}, f32[24,768]{1,0:T(8,128)S(1)}, u32[]{:S(2)}, u32[]{:S(2)}) collective-permute-start(f32[24,768]{1,0:T(8,128)S(1)} %step_piece.2.refs_0_.base_ref), channel_id=1, source_target_pairs={{0,2},{1,3},{2,0},{3,1},{4,6},{5,7},{6,4},{7,5},{8,10},{9,11},{10,... | collective-permute-start | bytes 221192 | tf_op jit(solution)/shard_map/ppermute | solution.py:62
  41.2 3.9 %collective-permute-done.14.refs_1_ = f32[24,768]{1,0:T(8,128)S(1)} collective-permute-done((f32[24,768]{1,0:T(8,128)S(1)}, f32[24,768]{1,0:T(8,128)S(1)}, u32[]{:S(2)}, u32[]{:S(2)}) %collective-permute-start.14) | collective-permute-done | bytes 73760 | tf_op jit(solution)/shard_map/ppermute | solution.py:62
  49.1 6.5 %collective-permute-done.17.refs_1_ = f32[96,768]{1,0:T(8,128)} collective-permute-done((f32[96,768]{1,0:T(8,128)S(1)}, f32[96,768]{1,0:T(8,128)}, u32[]{:S(2)}, u32[]{:S(2)}) %collective-permute-start.17) | collective-permute-done | bytes 294944 | tf_op jit(solution)/shard_map/ppermute | solution.py:62
  55.6 4.1 %collective-permute-done.18.refs_2_ = f32[96,768]{1,0:T(8,128)} collective-permute-done((f32[96,768]{1,0:T(8,128)S(1)}, f32[96,768]{1,0:T(8,128)}, u32[]{:S(2)}, u32[]{:S(2)}) %collective-permute-start.18) | collective-permute-done | bytes 294944 | tf_op jit(solution)/shard_map/ppermute | solution.py:62
  60.3 3.7 %all-to-all-start = ((f32[8,24,768]{2,1,0:T(8,128)}), f32[8,24,768]{2,1,0:T(8,128)S(1)}, u32[]{:S(2)}, u32[]{:S(2)}) async-start(f32[8,24,768]{2,1,0:T(8,128)} %bitcast.2), calls=%async_computation | async-start | bytes 1179648 | tf_op jit(solution)/shard_map/all_to_all | solution.py:328
  65.0 5.2 %apply.3 = (f32[96,768]{1,0:T(8,128)S(1)}, f32[96,768]{1,0:T(8,128)}) custom-call(f32[96,768]{1,0:T(8,128)S(1)} %stack.4.refs_0_, f32[96,768]{1,0:T(8,128)} %collective-permute-done.17.refs_1_, f32[96,768]{1,0:T(8,128)} %collective-permute-done.18.refs_2_, f32[96,768]{1,0:T(8,128)} %collective-permute-done.19.refs_3_, ...), custom_call_target="tpu_custom_call" | custom-call | tf_op jit(solution)/shard_map/apply/pallas_call | solution.py:119
  71.5 2.8 %all-to-all-done.pieces_ref = f32[8,24,768]{2,1,0:T(8,128)S(1)} async-done(((f32[8,24,768]{2,1,0:T(8,128)}), f32[8,24,768]{2,1,0:T(8,128)S(1)}, u32[]{:S(2)}, u32[]{:S(2)}) %all-to-all-start) | async-done | bytes 589856 | tf_op jit(solution)/shard_map/all_to_all | solution.py:328
  76.0 3.9 %all-to-all-start.1 = ((f32[8,24,768]{2,1,0:T(8,128)}), f32[8,24,768]{2,1,0:T(8,128)S(1)}, u32[]{:S(2)}, u32[]{:S(2)}) async-start(f32[8,24,768]{2,1,0:T(8,128)} %combine.1), calls=%async_computation.1 | async-start | bytes 1179648 | tf_op jit(solution)/shard_map/all_to_all | solution.py:330
  83.5 7.8 %collective-permute-done.25.refs_1_ = f32[24,768]{1,0:T(8,128)S(1)} collective-permute-done((f32[24,768]{1,0:T(8,128)S(1)}, f32[24,768]{1,0:T(8,128)S(1)}, u32[]{:S(2)}, u32[]{:S(2)}) %collective-permute-start.25) | collective-permute-done | bytes 73760 | tf_op jit(solution)/shard_map/ppermute | solution.py:62
  91.2 1.9 %collective-permute-done.27.refs_3_ = f32[24,768]{1,0:T(8,128)S(1)} collective-permute-done((f32[24,768]{1,0:T(8,128)S(1)}, f32[24,768]{1,0:T(8,128)S(1)}, u32[]{:S(2)}, u32[]{:S(2)}) %collective-permute-start.27) | collective-permute-done | bytes 73760 | tf_op jit(solution)/shard_map/ppermute | solution.py:62
  94.8 4.3 %collective-permute-start.29 = (f32[24,768]{1,0:T(8,128)S(1)}, f32[24,768]{1,0:T(8,128)S(1)}, u32[]{:S(2)}, u32[]{:S(2)}) collective-permute-start(f32[24,768]{1,0:T(8,128)S(1)} %step_piece.3.refs_0_), channel_id=1, source_target_pairs={{0,2},{1,3},{2,0},{3,1},{4,6},{5,7},{6,4},{7,5},{8,10},{9,11},{10,... | collective-permute-start | bytes 221192 | tf_op jit(solution)/shard_map/ppermute | solution.py:62
  100.1 3.1 %collective-permute-done.29.refs_2_ = f32[24,768]{1,0:T(8,128)S(1)} collective-permute-done((f32[24,768]{1,0:T(8,128)S(1)}, f32[24,768]{1,0:T(8,128)S(1)}, u32[]{:S(2)}, u32[]{:S(2)}) %collective-permute-start.29) | collective-permute-done | bytes 73760 | tf_op jit(solution)/shard_map/ppermute | solution.py:62
  104.6 2.5 %collective-permute-start.33 = (f32[96,768]{1,0:T(8,128)S(1)}, f32[96,768]{1,0:T(8,128)S(1)}, u32[]{:S(2)}, u32[]{:S(2)}) collective-permute-start(f32[96,768]{1,0:T(8,128)S(1)} %stack.5.refs_0_), channel_id=1, source_target_pairs={{0,24},{1,25},{2,26},{3,27},{4,28},{5,29},{6,30},{7,31},{8,16},{9,... | collective-permute-start | bytes 884744 | tf_op jit(solution)/shard_map/ppermute | solution.py:62
  107.0 6.4 %collective-permute-done.31.refs_1_ = f32[96,768]{1,0:T(8,128)S(1)} collective-permute-done((f32[96,768]{1,0:T(8,128)S(1)}, f32[96,768]{1,0:T(8,128)S(1)}, u32[]{:S(2)}, u32[]{:S(2)}) %collective-permute-start.31) | collective-permute-done | bytes 294944 | tf_op jit(solution)/shard_map/ppermute | solution.py:62
  114.6 2.3 %collective-permute-done.32.refs_2_ = f32[96,768]{1,0:T(8,128)S(1)} collective-permute-done((f32[96,768]{1,0:T(8,128)S(1)}, f32[96,768]{1,0:T(8,128)S(1)}, u32[]{:S(2)}, u32[]{:S(2)}) %collective-permute-start.32) | collective-permute-done | bytes 294944 | tf_op jit(solution)/shard_map/ppermute | solution.py:62
  116.9 3.3 %collective-permute-start.39 = (f32[192,768]{1,0:T(8,128)S(1)}, f32[192,768]{1,0:T(8,128)S(1)}, u32[]{:S(2)}, u32[]{:S(2)}) collective-permute-start(f32[192,768]{1,0:T(8,128)S(1)} %bitcast.7), channel_id=1, source_target_pairs={{0,2},{1,3},{2,0},{3,1},{4,6},{5,7},{6,4},{7,5},{8,10},{9,11},{10,... | collective-permute-start | bytes 1769480 | tf_op jit(solution)/shard_map/ppermute | solution.py:62
  122.2 24.1 %orthogonal.1 = (f32[192,768]{1,0:T(8,128)}, bf16[768,768]{1,0:T(8,128)(2,1)S(1)}, bf16[768,768]{1,0:T(8,128)(2,1)S(1)}) custom-call(f32[96,768]{1,0:T(8,128)S(1)} %stack.5.refs_0_, f32[96,768]{1,0:T(8,128)S(1)} %collective-permute-done.31.refs_1_, f32[96,768]{1,0:T(8,128)S(1)} %collective-permute-done.32.refs_2_, ...), custom_call_target="tpu_custom_call" | custom-call | tf_op jit(solution)/shard_map/orthogonal/pallas_call | solution.py:261
  146.3 12.8 %collective-permute-done.39.refs_2_ = f32[192,768]{1,0:T(8,128)S(1)} collective-permute-done((f32[192,768]{1,0:T(8,128)S(1)}, f32[192,768]{1,0:T(8,128)S(1)}, u32[]{:S(2)}, u32[]{:S(2)}) %collective-permute-start.39) | collective-permute-done | bytes 589856 | tf_op jit(solution)/shard_map/ppermute | solution.py:62
  159.1 9.2 %collective-permute-done.40.refs_3_ = f32[192,768]{1,0:T(8,128)S(1)} collective-permute-done((f32[192,768]{1,0:T(8,128)S(1)}, f32[192,768]{1,0:T(8,128)S(1)}, u32[]{:S(2)}, u32[]{:S(2)}) %collective-permute-start.40) | collective-permute-done | bytes 589856 | tf_op jit(solution)/shard_map/ppermute | solution.py:62
  168.3 3.5 %environment.1 = f32[192,768]{1,0:T(8,128)} custom-call(f32[192,768]{1,0:T(8,128)S(1)} %bitcast.9, f32[192,768]{1,0:T(8,128)S(1)} %collective-permute-done.38.refs_1_, f32[192,768]{1,0:T(8,128)S(1)} %collective-permute-done.39.refs_2_, f32[192,768]{1,0:T(8,128)S(1)} %collective-permute-done.40.refs_3_, bf16[768,768]{1,0:T(8,128)(2,1)S(1)} %get-tuple-element.48.refs_4_, ...), custom_call_target="tpu_custom_call" | custom-call | tf_op jit(solution)/shard_map/environment/pallas_call | solution.py:288
  (102 shorter events, 42.3 us)
Async XLA Ops:
  10.8 8.4 %collective-permute-start.3 = (f32[72,768]{1,0:T(8,128)S(1)}, f32[72,768]{1,0:T(8,128)S(1)}, u32[]{:S(2)}, u32[]{:S(2)}) collective-permute-start(f32[72,768]{1,0:T(8,128)S(1)} %stack.3.refs_1_), channel_id=1, source_target_pairs={{0,8},{1,9},{2,10},{3,11},{4,12},{5,13},{6,14},{7,15},{8,0},{9,1},... | collective-permute-start | bytes 663560 | tf_op jit(solution)/shard_map/ppermute | solution.py:62
  12.4 10.5 %collective-permute-start.4 = (f32[72,768]{1,0:T(8,128)S(1)}, f32[72,768]{1,0:T(8,128)S(1)}, u32[]{:S(2)}, u32[]{:S(2)}) collective-permute-start(f32[72,768]{1,0:T(8,128)S(1)} %stack.3.refs_1_), channel_id=1, source_target_pairs={{0,16},{1,17},{2,18},{3,19},{4,20},{5,21},{6,22},{7,23},{8,24},{9,... | collective-permute-start | bytes 663560 | tf_op jit(solution)/shard_map/ppermute | solution.py:62
  13.9 9.0 %collective-permute-start.5 = (f32[72,768]{1,0:T(8,128)S(1)}, f32[72,768]{1,0:T(8,128)S(1)}, u32[]{:S(2)}, u32[]{:S(2)}) collective-permute-start(f32[72,768]{1,0:T(8,128)S(1)} %stack.3.refs_1_), channel_id=1, source_target_pairs={{0,24},{1,25},{2,26},{3,27},{4,28},{5,29},{6,30},{7,31},{8,16},{9,... | collective-permute-start | bytes 663560 | tf_op jit(solution)/shard_map/ppermute | solution.py:62
  14.4 9.1 %collective-permute-start.6 = (f32[72,768]{1,0:T(8,128)S(1)}, f32[72,768]{1,0:T(8,128)S(1)}, u32[]{:S(2)}, u32[]{:S(2)}) collective-permute-start(f32[72,768]{1,0:T(8,128)S(1)} %stack.3.refs_1_), channel_id=1, source_target_pairs={{0,4},{1,5},{2,6},{3,7},{4,0},{5,1},{6,2},{7,3},{8,12},{9,13},{10,... | collective-permute-start | bytes 663560 | tf_op jit(solution)/shard_map/ppermute | solution.py:62
  36.8 8.2 %collective-permute-start.14 = (f32[24,768]{1,0:T(8,128)S(1)}, f32[24,768]{1,0:T(8,128)S(1)}, u32[]{:S(2)}, u32[]{:S(2)}) collective-permute-start(f32[24,768]{1,0:T(8,128)S(1)} %step_piece.2.refs_0_.base_ref), channel_id=1, source_target_pairs={{0,3},{1,2},{2,1},{3,0},{4,7},{5,6},{6,5},{7,4},{8,11},{9,10},{10,... | collective-permute-start | bytes 221192 | tf_op jit(solution)/shard_map/ppermute | solution.py:62
  45.5 10.0 %collective-permute-start.17 = (f32[96,768]{1,0:T(8,128)S(1)}, f32[96,768]{1,0:T(8,128)}, u32[]{:S(2)}, u32[]{:S(2)}) collective-permute-start(f32[96,768]{1,0:T(8,128)S(1)} %stack.4.refs_0_), channel_id=1, source_target_pairs={{0,8},{1,9},{2,10},{3,11},{4,12},{5,13},{6,14},{7,15},{8,0},{9,1},... | collective-permute-start | bytes 884744 | tf_op jit(solution)/shard_map/ppermute | solution.py:62
  47.1 12.6 %collective-permute-start.18 = (f32[96,768]{1,0:T(8,128)S(1)}, f32[96,768]{1,0:T(8,128)}, u32[]{:S(2)}, u32[]{:S(2)}) collective-permute-start(f32[96,768]{1,0:T(8,128)S(1)} %stack.4.refs_0_), channel_id=1, source_target_pairs={{0,16},{1,17},{2,18},{3,19},{4,20},{5,21},{6,22},{7,23},{8,24},{9,... | collective-permute-start | bytes 884744 | tf_op jit(solution)/shard_map/ppermute | solution.py:62
  47.8 12.0 %collective-permute-start.19 = (f32[96,768]{1,0:T(8,128)S(1)}, f32[96,768]{1,0:T(8,128)}, u32[]{:S(2)}, u32[]{:S(2)}) collective-permute-start(f32[96,768]{1,0:T(8,128)S(1)} %stack.4.refs_0_), channel_id=1, source_target_pairs={{0,24},{1,25},{2,26},{3,27},{4,28},{5,29},{6,30},{7,31},{8,16},{9,... | collective-permute-start | bytes 884744 | tf_op jit(solution)/shard_map/ppermute | solution.py:62
  49.1 14.9 %collective-permute-start.20 = (f32[96,768]{1,0:T(8,128)S(1)}, f32[96,768]{1,0:T(8,128)}, u32[]{:S(2)}, u32[]{:S(2)}) collective-permute-start(f32[96,768]{1,0:T(8,128)S(1)} %stack.4.refs_0_), channel_id=1, source_target_pairs={{0,4},{1,5},{2,6},{3,7},{4,0},{5,1},{6,2},{7,3},{8,12},{9,13},{10,... | collective-permute-start | bytes 884744 | tf_op jit(solution)/shard_map/ppermute | solution.py:62
  55.6 8.4 %collective-permute-start.21 = (f32[96,768]{1,0:T(8,128)}, f32[96,768]{1,0:T(8,128)}, u32[]{:S(2)}, u32[]{:S(2)}) collective-permute-start(f32[96,768]{1,0:T(8,128)} %collective-permute-done.17.refs_1_), channel_id=1, source_target_pairs={{0,4},{1,5},{2,6},{3,7},{4,0},{5,1},{6,2},{7,3},{8,12},{9,13},{10,... | collective-permute-start | bytes 884744 | tf_op jit(solution)/shard_map/ppermute | solution.py:62
  60.3 14.0 %all-to-all-start = ((f32[8,24,768]{2,1,0:T(8,128)}), f32[8,24,768]{2,1,0:T(8,128)S(1)}, u32[]{:S(2)}, u32[]{:S(2)}) async-start(f32[8,24,768]{2,1,0:T(8,128)} %bitcast.2), calls=%async_computation | async-start | bytes 1179648 | tf_op jit(solution)/shard_map/all_to_all | solution.py:328
  70.9 8.9 %collective-permute-start.24 = (f32[96,768]{1,0:T(8,128)}, f32[96,768]{1,0:T(8,128)S(1)}, u32[]{:S(2)}, u32[]{:S(2)}) collective-permute-start(f32[96,768]{1,0:T(8,128)} %get-tuple-element.42), channel_id=1, source_target_pairs={{0,4},{1,5},{2,6},{3,7},{4,0},{5,1},{6,2},{7,3},{8,12},{9,13},{10,... | collective-permute-start | bytes 884744 | tf_op jit(solution)/shard_map/ppermute | solution.py:62
  76.0 37.4 %all-to-all-start.1 = ((f32[8,24,768]{2,1,0:T(8,128)}), f32[8,24,768]{2,1,0:T(8,128)S(1)}, u32[]{:S(2)}, u32[]{:S(2)}) async-start(f32[8,24,768]{2,1,0:T(8,128)} %combine.1), calls=%async_computation.1 | async-start | bytes 1179648 | tf_op jit(solution)/shard_map/all_to_all | solution.py:330
  79.9 11.3 %collective-permute-start.25 = (f32[24,768]{1,0:T(8,128)S(1)}, f32[24,768]{1,0:T(8,128)S(1)}, u32[]{:S(2)}, u32[]{:S(2)}) collective-permute-start(f32[24,768]{1,0:T(8,128)S(1)} %get-tuple-element.44), channel_id=1, source_target_pairs={{0,8},{1,9},{2,10},{3,11},{4,12},{5,13},{6,14},{7,15},{8,0},{9,1},... | collective-permute-start | bytes 221192 | tf_op jit(solution)/shard_map/ppermute | solution.py:62
  81.7 9.5 %collective-permute-start.26 = (f32[24,768]{1,0:T(8,128)S(1)}, f32[24,768]{1,0:T(8,128)S(1)}, u32[]{:S(2)}, u32[]{:S(2)}) collective-permute-start(f32[24,768]{1,0:T(8,128)S(1)} %get-tuple-element.45), channel_id=1, source_target_pairs={{0,16},{1,17},{2,18},{3,19},{4,20},{5,21},{6,22},{7,23},{8,24},{9,... | collective-permute-start | bytes 221192 | tf_op jit(solution)/shard_map/ppermute | solution.py:62
  83.2 10.0 %collective-permute-start.27 = (f32[24,768]{1,0:T(8,128)S(1)}, f32[24,768]{1,0:T(8,128)S(1)}, u32[]{:S(2)}, u32[]{:S(2)}) collective-permute-start(f32[24,768]{1,0:T(8,128)S(1)} %get-tuple-element.46), channel_id=1, source_target_pairs={{0,24},{1,25},{2,26},{3,27},{4,28},{5,29},{6,30},{7,31},{8,16},{9,... | collective-permute-start | bytes 221192 | tf_op jit(solution)/shard_map/ppermute | solution.py:62
  94.8 8.3 %collective-permute-start.29 = (f32[24,768]{1,0:T(8,128)S(1)}, f32[24,768]{1,0:T(8,128)S(1)}, u32[]{:S(2)}, u32[]{:S(2)}) collective-permute-start(f32[24,768]{1,0:T(8,128)S(1)} %step_piece.3.refs_0_), channel_id=1, source_target_pairs={{0,2},{1,3},{2,0},{3,1},{4,6},{5,7},{6,4},{7,5},{8,10},{9,11},{10,... | collective-permute-start | bytes 221192 | tf_op jit(solution)/shard_map/ppermute | solution.py:62
  103.5 9.9 %collective-permute-start.31 = (f32[96,768]{1,0:T(8,128)S(1)}, f32[96,768]{1,0:T(8,128)S(1)}, u32[]{:S(2)}, u32[]{:S(2)}) collective-permute-start(f32[96,768]{1,0:T(8,128)S(1)} %stack.5.refs_0_), channel_id=1, source_target_pairs={{0,8},{1,9},{2,10},{3,11},{4,12},{5,13},{6,14},{7,15},{8,0},{9,1},... | collective-permute-start | bytes 884744 | tf_op jit(solution)/shard_map/ppermute | solution.py:62
  104.1 12.8 %collective-permute-start.32 = (f32[96,768]{1,0:T(8,128)S(1)}, f32[96,768]{1,0:T(8,128)S(1)}, u32[]{:S(2)}, u32[]{:S(2)}) collective-permute-start(f32[96,768]{1,0:T(8,128)S(1)} %stack.5.refs_0_), channel_id=1, source_target_pairs={{0,16},{1,17},{2,18},{3,19},{4,20},{5,21},{6,22},{7,23},{8,24},{9,... | collective-permute-start | bytes 884744 | tf_op jit(solution)/shard_map/ppermute | solution.py:62
  104.6 15.6 %collective-permute-start.33 = (f32[96,768]{1,0:T(8,128)S(1)}, f32[96,768]{1,0:T(8,128)S(1)}, u32[]{:S(2)}, u32[]{:S(2)}) collective-permute-start(f32[96,768]{1,0:T(8,128)S(1)} %stack.5.refs_0_), channel_id=1, source_target_pairs={{0,24},{1,25},{2,26},{3,27},{4,28},{5,29},{6,30},{7,31},{8,16},{9,... | collective-permute-start | bytes 884744 | tf_op jit(solution)/shard_map/ppermute | solution.py:62
  107.0 13.1 %collective-permute-start.34 = (f32[96,768]{1,0:T(8,128)S(1)}, f32[96,768]{1,0:T(8,128)S(1)}, u32[]{:S(2)}, u32[]{:S(2)}) collective-permute-start(f32[96,768]{1,0:T(8,128)S(1)} %stack.5.refs_0_), channel_id=1, source_target_pairs={{0,4},{1,5},{2,6},{3,7},{4,0},{5,1},{6,2},{7,3},{8,12},{9,13},{10,... | collective-permute-start | bytes 884744 | tf_op jit(solution)/shard_map/ppermute | solution.py:62
  113.4 32.9 %collective-permute-start.38 = (f32[192,768]{1,0:T(8,128)S(1)}, f32[192,768]{1,0:T(8,128)S(1)}, u32[]{:S(2)}, u32[]{:S(2)}) collective-permute-start(f32[192,768]{1,0:T(8,128)S(1)} %bitcast.6), channel_id=1, source_target_pairs={{0,1},{1,0},{2,3},{3,2},{4,5},{5,4},{6,7},{7,6},{8,9},{9,8},{10,11... | collective-permute-start | bytes 1769480 | tf_op jit(solution)/shard_map/ppermute | solution.py:62
  116.9 42.3 %collective-permute-start.39 = (f32[192,768]{1,0:T(8,128)S(1)}, f32[192,768]{1,0:T(8,128)S(1)}, u32[]{:S(2)}, u32[]{:S(2)}) collective-permute-start(f32[192,768]{1,0:T(8,128)S(1)} %bitcast.7), channel_id=1, source_target_pairs={{0,2},{1,3},{2,0},{3,1},{4,6},{5,7},{6,4},{7,5},{8,10},{9,11},{10,... | collective-permute-start | bytes 1769480 | tf_op jit(solution)/shard_map/ppermute | solution.py:62
  120.2 48.2 %collective-permute-start.40 = (f32[192,768]{1,0:T(8,128)S(1)}, f32[192,768]{1,0:T(8,128)S(1)}, u32[]{:S(2)}, u32[]{:S(2)}) collective-permute-start(f32[192,768]{1,0:T(8,128)S(1)} %bitcast.8), channel_id=1, source_target_pairs={{0,3},{1,2},{2,1},{3,0},{4,7},{5,6},{6,5},{7,4},{8,11},{9,10},{10,... | collective-permute-start | bytes 1769480 | tf_op jit(solution)/shard_map/ppermute | solution.py:62
  (31 other events, 225.7 us)
where the time goes:
time: 172 us
  waiting for transfers between devices  81 us (47%)
  starting transfers between devices  46.3 us (27%)
  Pallas kernels  39.3 us (23%)
  local copies, waits for them, and re-layouts  4.43 us (3%)
    ppermute x41, waiting for transfers between devices, swap(): return lax.ppermute(value, ('terms', 'rows'), pairs)  78.1 us
    ppermute x41, starting transfers between devices, swap(): return lax.ppermute(value, ('terms', 'rows'), pairs)  38.8 us
    pallas_call x1, Pallas kernels, orthogonal(): pl.pallas_call(kernel, out_shape=(shape((slab, width)),) + (shape(square,...  24.1 us
    pallas_call x2, Pallas kernels, apply_terms(): pl.pallas_call(kernel, out_shape=(shape((half, width)),) * 2, in_specs=[V...  8.28 us
    all_to_all x1, starting transfers between devices, combined_slab(): lax.all_to_all(mixed, 'terms', 0, 0, tiled=True).reshape(rows, width)  3.85 us
    all_to_all x1, starting transfers between devices, combined_slab(): lax.all_to_all(left.reshape((owners,) + run), 'terms', 0, 0, tiled=True)  3.68 us
    pallas_call x1, Pallas kernels, environment(): pl.pallas_call(kernel, out_shape=shape((slab, width)), in_specs=[VMEM] *...  3.54 us
    unnamed x26, local copies, waits for them, and re-layouts  3.54 us
  transfers between devices with their start and end apart: 43, of which 27 were waited for; matrix products, arithmetic and copies ran while one was open for 0% of the time, Pallas kernels for 19%

commit v1 on v0

--- a/solution.py
+++ b/solution.py
@@ -62,28 +62,123 @@
         return lax.ppermute(value, ("terms", "rows"), pairs)
 
 
-def prepare(places, left, right):
+def order_left(places, left):
+    width = left.shape[1]
     piece, half = places.piece, places.half
 
-    def kernel(left_ref, right_ref, lh_ref, ll_ref, rh_ref, rl_ref, ordered):
+    def kernel(left_ref, own_ref, away_ref, lh_ref, ll_ref):
         chip, core, _ = places.here()
+        for side, out in enumerate((own_ref, away_ref)):
+            for slot in range(places.chips):
+                source = pl.multiple_of((core ^ side) * half + (chip ^ slot) * piece, 8)
+                out[pl.ds(slot * piece, piece), :] = left_ref[pl.ds(source, piece), :]
+            rows = pl.ds(side * half, half)
+            lh_ref[rows, :], ll_ref[rows, :] = halves(out[...])
+
+    return pl.pallas_call(
+        kernel,
+        out_shape=(shape((half, width)),) * 2 + (shape(left.shape, BF16),) * 2,
+        in_specs=[VMEM],
+        out_specs=(VMEM,) * 4,
+        compiler_params=pltpu.CompilerParams(vmem_limit_bytes=4 * MIB),
+        name="order_left",
+    )(left)
+
+
+def split_right(right):
+    def kernel(right_ref, rh_ref, rl_ref):
+        rh_ref[...], rl_ref[...] = halves(right_ref[...])
+
+    return pl.pallas_call(
+        kernel,
+        out_shape=(shape(right.shape, BF16),) * 2,
+        in_specs=[VMEM],
+        out_specs=(VMEM,) * 2,
+        compiler_params=pltpu.CompilerParams(vmem_limit_bytes=4 * MIB),
+        name="split_right",
+    )(right)
+
+
+def pair_pieces(places, own, received):
+    piece = places.piece
+    width = own.shape[1]
+
+    def kernel(own_ref, received_ref, *outs):
+        for slot, out in enumerate(outs):
+            rows = pl.ds(slot * piece, piece)
+            out[pl.ds(0, piece), :] = own_ref[rows, :]
+            out[pl.ds(piece, piece), :] = received_ref[rows, :]
+
+    return pl.pallas_call(
+        kernel,
+        out_shape=(shape((2 * piece, width)),) * places.chips,
+        in_specs=[VMEM, VMEM],
+        out_specs=(VMEM,) * places.chips,
+        compiler_params=pltpu.CompilerParams(vmem_limit_bytes=2 * MIB),
+        name="pair_pieces",
+    )(own, received)
+
+
+def exchange(places, own, away):
+    received = places.swap(away, core=1)
+    first, *others = pair_pieces(places, own, received)
+    return [first] + [places.swap(part, chip=slot + 1) for slot, part in enumerate(others)]
+
+
+def by_source(places, parts, whole, stride):
+    chip, core, _ = places.here()
+    piece = places.piece
+    for slot, part in enumerate(parts):
         for side in range(places.cores):
+            start = pl.multiple_of((chip ^ slot) * stride[0] + (core ^ side) * stride[1], 8)
+            whole[pl.ds(start, piece), :] = part[pl.ds(side * piece, piece), :]
+
+
+def combine_exchanged(places, parts, source_list, list_count, weight_index, weight_table):
+    fan = source_list.shape[1]
+    width = parts[0].shape[1]
+    piece, half = places.piece, places.half
+
+    def kernel(source_ref, count_ref, index_ref, table_ref, *refs):
+        *ins, own_ref, away_ref, whole = refs
+        by_source(places, ins, whole, (places.cores * piece, piece))
+        chip, core, _ = places.here()
+        for side, out in enumerate((own_ref, away_ref)):
             for slot in range(places.chips):
-                source = (core ^ side) * half + (chip ^ slot) * piece
-                source = pl.multiple_of(source, 8)
-                ordered[pl.ds(side * half + slot * piece, piece), :] = left_ref[pl.ds(source, piece), :]
-        lh_ref[...], ll_ref[...] = halves(ordered[...])
-        rh_ref[...], rl_ref[...] = halves(right_ref[...])
-
-    return pl.pallas_call(
-        kernel,
-        out_shape=(shape(left.shape, BF16),) * 2 + (shape(right.shape, BF16),) * 2,
-        in_specs=[VMEM, VMEM],
-        out_specs=(VMEM,) * 4,
-        scratch_shapes=[pltpu.VMEM(left.shape, F32)],
-        compiler_params=pltpu.CompilerParams(vmem_limit_bytes=12 * MIB),
-        name="prepare",
-    )(left, right)
+                j = (chip ^ slot) * places.cores + (core ^ side)
+                total = None
+                for c in range(fan):
+                    weight = jnp.where(c < count_ref[j], table_ref[index_ref[j, c]], 0.0)
+                    start = pl.multiple_of(source_ref[j, c] * piece, 8)
+                    term = weight * whole[pl.ds(start, piece), :]
+                    total = term if total is None else total + term
+                out[pl.ds(slot * piece, piece), :] = total
+
+    return pl.pallas_call(
+        kernel,
+        out_shape=(shape((half, width)),) * 2,
+        in_specs=[SMEM] * 4 + [VMEM] * len(parts),
+        out_specs=(VMEM, VMEM),
+        scratch_shapes=[pltpu.VMEM((places.slab, width), F32)],
+        compiler_params=pltpu.CompilerParams(vmem_limit_bytes=4 * MIB),
+        name="combine",
+    )(source_list, list_count, weight_index, weight_table, *parts)
+
+
+def place_rows(places, parts):
+    width = parts[0].shape[1]
+
+    def kernel(*refs):
+        by_source(places, refs[:-1], refs[-1], (places.piece, places.half))
+
+    return pl.pallas_call(
+        kernel,
+        out_shape=shape((places.slab, width)),
+        in_specs=[VMEM] * len(parts),
+        out_specs=VMEM,
+        compiler_params=pltpu.CompilerParams(vmem_limit_bytes=2 * MIB),
+        name="place_rows",
+    )(*parts)
 
 
 def assemble(places, layout, parts, store):
@@ -122,7 +217,7 @@
         in_specs=[VMEM] * (len(parts) + 4),
         out_specs=(VMEM, VMEM),
         scratch_shapes=[pltpu.VMEM((width, width), F32)],
-        compiler_params=pltpu.CompilerParams(vmem_limit_bytes=16 * MIB),
+        compiler_params=pltpu.CompilerParams(vmem_limit_bytes=10 * MIB),
         name="apply",
     )(*parts, *prepared)
 
@@ -146,18 +241,20 @@
     )(keep, received)
 
 
-def step_piece(base, pieces):
+def step_piece(base, pieces, copies):
     def kernel(base_ref, *refs):
-        total = refs[0][...]
-        for ref in refs[1:-1]:
+        ins, outs = refs[: len(pieces)], refs[len(pieces) :]
+        total = ins[0][...]
+        for ref in ins[1:]:
             total = total + ref[...]
-        refs[-1][...] = base_ref[...] - STEP * total
-
-    return pl.pallas_call(
-        kernel,
-        out_shape=shape(base.shape),
+        for out in outs:
+            out[...] = base_ref[...] - STEP * total
+
+    return pl.pallas_call(
+        kernel,
+        out_shape=(shape(base.shape),) * copies,
         in_specs=[VMEM] * (1 + len(pieces)),
-        out_specs=VMEM,
+        out_specs=(VMEM,) * copies,
         compiler_params=pltpu.CompilerParams(vmem_limit_bytes=2 * MIB),
         name="step_piece",
     )(base, *pieces)
@@ -264,7 +361,7 @@
         in_specs=[VMEM] * len(parts),
         out_specs=(VMEM,) * 3,
         scratch_shapes=[pltpu.VMEM(square, F32)] * 3 + [pltpu.VMEM(square, BF16)] * 4,
-        compiler_params=pltpu.CompilerParams(vmem_limit_bytes=40 * MIB),
+        compiler_params=pltpu.CompilerParams(vmem_limit_bytes=24 * MIB),
         name="orthogonal",
     )(*parts)
 
@@ -291,7 +388,7 @@
         in_specs=[VMEM] * (len(parts) + 2),
         out_specs=VMEM,
         scratch_shapes=[pltpu.VMEM((width, width), BF16)] * 2,
-        compiler_params=pltpu.CompilerParams(vmem_limit_bytes=16 * MIB),
+        compiler_params=pltpu.CompilerParams(vmem_limit_bytes=10 * MIB),
         name="environment",
     )(*parts, high, low)
 
@@ -327,7 +424,7 @@
         run = (1, rows * width // owners)
     pieces = lax.all_to_all(left.reshape((owners,) + run), "terms", 0, 0, tiled=True)
     mixed = combine_pieces(pieces, source_list, list_count, weight_index, weight_table)
-    return mixed, lax.all_to_all(mixed, "terms", 0, 0, tiled=True).reshape(rows, width)
+    return lax.all_to_all(mixed, "terms", 0, 0, tiled=True).reshape(rows, width)
 
 
 def body(amplitudes, left_terms, right_terms, source_list, list_count, weight_index, weight_table):
@@ -336,20 +433,25 @@
     terms, rows = lax.axis_size("terms"), lax.axis_size("rows")
     places = Places(terms, rows, slab)
 
-    _, combined = combined_slab(left, source_list, list_count, weight_index, weight_table)
+    lists = (source_list, list_count, weight_index, weight_table)
     chip, core, line = places.here()
     every = list(range(rows))
     slabs = [(0, 0, [slot], slab) for slot in every]
     if swappable(terms, rows, slab):
-        prepared = prepare(places, left, right)
+        own, away, *left_halves = order_left(places, left)
+        prepared = (*left_halves, *split_right(right))
+        pieces = exchange(places, own, away)
+        own, away = combine_exchanged(places, pieces, *lists)
+        combined = place_rows(places, exchange(places, own, away))
         start = core * places.half + chip * places.piece
         base = lax.dynamic_slice_in_dim(amplitudes, start, places.piece, 0)
         layout, parts, prepared = spread(places, base, with_own=False, ready=prepared)
         layout, parts = [slabs[0]] + layout, [amplitudes] + parts
-        for _ in range(2):
+        for name in ("f", "x"):
             keep, send = apply_terms(places, layout, parts, prepared)
-            base = step_piece(base, reduced(places, keep, send))
-            layout, parts, _ = spread(places, base)
+            sent, *kept = step_piece(base, reduced(places, keep, send), 2 if name == "f" else 1)
+            layout, parts, _ = spread(places, sent)
+            base = kept[0] if kept else None
         blocks = [combined]
         for slot in every[1:]:
             blocks.append(places.swap(combined, row=slot))
@@ -363,6 +465,7 @@
         full = lax.all_gather(matrix, "rows", axis=0, tiled=True)
         layout = slabs
         parts = [lax.dynamic_slice_in_dim(full, (line ^ slot) * slab, slab, 0) for slot in every]
+        combined = combined_slab(left, *lists)
         full = lax.all_gather(combined, "rows", axis=0, tiled=True)
         blocks = [lax.dynamic_slice_in_dim(full, (line ^ slot) * slab, slab, 0) for slot in every]
     isometry, high, low = orthogonal(places, layout, parts)

time: 172 us -> 170 us (0.988)
  Pallas kernels: 39.3 us -> 35.6 us
  waiting for transfers between devices: 81 us -> 84.1 us
    all_to_all x2 -> x0, starting transfers between devices: 7.53 us -> none  [the longest x1 3.85 us: combined_slab(): lax.all_to_all(mixed, 'terms', 0, 0, tiled=True).reshape(rows, width)]
    ppermute x41 -> x49, starting transfers between devices: 38.8 us -> 45.2 us  [swap(): return lax.ppermute(value, ('terms', 'rows'), pairs)]
    ppermute x41 -> x49, waiting for transfers between devices: 78.1 us -> 84.1 us  [swap(): return lax.ppermute(value, ('terms', 'rows'), pairs)]
    all_to_all x2 -> x0, waiting for transfers between devices: 2.82 us -> none  [the longest x1 2.81 us: combined_slab(): lax.all_to_all(left.reshape((owners,) + run), 'terms', 0, 0, tiled=True)]
    pallas_call x2, Pallas kernels: 8.28 us -> 6.06 us  [apply_terms(): pl.pallas_call(kernel, out_shape=(shape((half, width)),) * 2, in_specs=[V...]
    unnamed x26 -> x16, local copies, waits for them, and re-layouts: 3.54 us -> 2.91 us
  transfers between devices with their start and end apart: 43 -> 49, of which waited for: 27 -> 26; matrix products, arithmetic and copies ran while one was open for 0% -> 0% of each run, Pallas kernels for 19% -> 17%
where the time goes in v1:
time: 170 us
  waiting for transfers between devices  84.1 us (49%)
  starting transfers between devices  45.2 us (27%)
  Pallas kernels  35.6 us (21%)
  local copies, waits for them, and re-layouts  3.8 us (2%)
    ppermute x49, waiting for transfers between devices, swap(): return lax.ppermute(value, ('terms', 'rows'), pairs)  84.1 us
    ppermute x49, starting transfers between devices, swap(): return lax.ppermute(value, ('terms', 'rows'), pairs)  45.2 us
    pallas_call x1, Pallas kernels, orthogonal(): pl.pallas_call(kernel, out_shape=(shape((slab, width)),) + (shape(square,...  24.3 us
    pallas_call x2, Pallas kernels, apply_terms(): pl.pallas_call(kernel, out_shape=(shape((half, width)),) * 2, in_specs=[V...  6.06 us
    pallas_call x1, Pallas kernels, environment(): pl.pallas_call(kernel, out_shape=shape((slab, width)), in_specs=[VMEM] *...  3.54 us
  transfers between devices with their start and end apart: 49, of which 26 were waited for; matrix products, arithmetic and copies ran while one was open for 0% of the time, Pallas kernels for 17%

profile of v1, /device:TPU:8, one launch (start us, length us, event | category | flops | bytes accessed | tf_op | source)
XLA Modules:
  0.0 169.6 jit_solution(11851950544184225889)
XLA Ops:
  6.9 1.7 copy-done
  14.4 4.8 %collective-permute-done.3.refs_2_ = f32[72,768]{1,0:T(8,128)S(1)} collective-permute-done((f32[72,768]{1,0:T(8,128)S(1)}, f32[72,768]{1,0:T(8,128)S(1)}, u32[]{:S(2)}, u32[]{:S(2)}) %collective-permute-start.3) | collective-permute-done | bytes 221216 | tf_op jit(solution)/shard_map/ppermute | solution.py:62
  19.2 3.7 %collective-permute-done.4.refs_3_ = f32[72,768]{1,0:T(8,128)S(1)} collective-permute-done((f32[72,768]{1,0:T(8,128)S(1)}, f32[72,768]{1,0:T(8,128)S(1)}, u32[]{:S(2)}, u32[]{:S(2)}) %collective-permute-start.4) | collective-permute-done | bytes 221216 | tf_op jit(solution)/shard_map/ppermute | solution.py:62
  24.7 3.0 %apply.2 = (f32[96,768]{1,0:T(8,128)S(1)}, f32[96,768]{1,0:T(8,128)S(1)}) custom-call(f32[192,768]{1,0:T(8,128)S(1)} %copy-done.1, f32[72,768]{1,0:T(8,128)S(1)} %stack.3.refs_1_, f32[72,768]{1,0:T(8,128)S(1)} %collective-permute-done.3.refs_2_, f32[72,768]{1,0:T(8,128)S(1)} %collective-permute-done.4.refs_3_, f32[72,768]{1,0:T(8,128)S(1)} %collective-permute-done.5.refs_4_, ...), custom_call_target="tpu_custom_call" | custom-call | tf_op jit(solution)/shard_map/apply/pallas_call | solution.py:214
  34.8 2.0 %collective-permute-done.13.refs_3_ = f32[24,768]{1,0:T(8,128)S(1)} collective-permute-done((f32[24,768]{1,0:T(8,128)S(1)}, f32[24,768]{1,0:T(8,128)S(1)}, u32[]{:S(2)}, u32[]{:S(2)}) %collective-permute-start.13) | collective-permute-done | bytes 73760 | tf_op jit(solution)/shard_map/ppermute | solution.py:62
  37.2 3.9 %collective-permute-start.15 = (f32[24,768]{1,0:T(8,128)S(1)}, f32[24,768]{1,0:T(8,128)S(1)}, u32[]{:S(2)}, u32[]{:S(2)}) collective-permute-start(f32[24,768]{1,0:T(8,128)S(1)} %get-tuple-element.56.refs_0_), channel_id=1, source_target_pairs={{0,2},{1,3},{2,0},{3,1},{4,6},{5,7},{6,4},{7,5},{8,10},{9,11},{10,... | collective-permute-start | bytes 221192 | tf_op jit(solution)/shard_map/ppermute | solution.py:62
  41.1 3.9 %collective-permute-done.14.refs_1_ = f32[24,768]{1,0:T(8,128)S(1)} collective-permute-done((f32[24,768]{1,0:T(8,128)S(1)}, f32[24,768]{1,0:T(8,128)S(1)}, u32[]{:S(2)}, u32[]{:S(2)}) %collective-permute-start.14) | collective-permute-done | bytes 73760 | tf_op jit(solution)/shard_map/ppermute | solution.py:62
  49.6 5.9 %collective-permute-done.17.refs_1_ = f32[96,768]{1,0:T(8,128)S(1)} collective-permute-done((f32[96,768]{1,0:T(8,128)S(1)}, f32[96,768]{1,0:T(8,128)S(1)}, u32[]{:S(2)}, u32[]{:S(2)}) %collective-permute-start.17) | collective-permute-done | bytes 294944 | tf_op jit(solution)/shard_map/ppermute | solution.py:62
  55.5 4.1 %collective-permute-done.18.refs_2_ = f32[96,768]{1,0:T(8,128)S(1)} collective-permute-done((f32[96,768]{1,0:T(8,128)S(1)}, f32[96,768]{1,0:T(8,128)S(1)}, u32[]{:S(2)}, u32[]{:S(2)}) %collective-permute-start.18) | collective-permute-done | bytes 294944 | tf_op jit(solution)/shard_map/ppermute | solution.py:62
  61.6 3.0 %apply.3 = (f32[96,768]{1,0:T(8,128)S(1)}, f32[96,768]{1,0:T(8,128)S(1)}) custom-call(f32[96,768]{1,0:T(8,128)S(1)} %stack.4.refs_0_, f32[96,768]{1,0:T(8,128)S(1)} %collective-permute-done.17.refs_1_, f32[96,768]{1,0:T(8,128)S(1)} %collective-permute-done.18.refs_2_, f32[96,768]{1,0:T(8,128)S(1)} %collective-permute-done.19.refs_3_, ...), custom_call_target="tpu_custom_call" | custom-call | tf_op jit(solution)/shard_map/apply/pallas_call | solution.py:214
  64.9 2.2 %collective-permute-start.41 = (f32[48,768]{1,0:T(8,128)S(1)}, f32[48,768]{1,0:T(8,128)S(1)}, u32[]{:S(2)}, u32[]{:S(2)}) collective-permute-start(f32[48,768]{1,0:T(8,128)S(1)} %get-tuple-element.69), channel_id=1, source_target_pairs={{0,24},{1,25},{2,26},{3,27},{4,28},{5,29},{6,30},{7,31},{8,16},{9,... | collective-permute-start | bytes 442376 | tf_op jit(solution)/shard_map/ppermute | solution.py:62
  67.2 4.7 %collective-permute-done.41.refs_3_ = f32[48,768]{1,0:T(8,128)S(1)} collective-permute-done((f32[48,768]{1,0:T(8,128)S(1)}, f32[48,768]{1,0:T(8,128)S(1)}, u32[]{:S(2)}, u32[]{:S(2)}) %collective-permute-start.41) | collective-permute-done | bytes 147488 | tf_op jit(solution)/shard_map/ppermute | solution.py:62
  72.9 1.7 %collective-permute-start.25 = (f32[24,768]{1,0:T(8,128)S(1)}, f32[24,768]{1,0:T(8,128)S(1)}, u32[]{:S(2)}, u32[]{:S(2)}) collective-permute-start(f32[24,768]{1,0:T(8,128)S(1)} %get-tuple-element.60), channel_id=1, source_target_pairs={{0,8},{1,9},{2,10},{3,11},{4,12},{5,13},{6,14},{7,15},{8,0},{9,1},... | collective-permute-start | bytes 221192 | tf_op jit(solution)/shard_map/ppermute | solution.py:62
  79.0 2.0 %collective-permute-done.27.refs_3_ = f32[24,768]{1,0:T(8,128)S(1)} collective-permute-done((f32[24,768]{1,0:T(8,128)S(1)}, f32[24,768]{1,0:T(8,128)S(1)}, u32[]{:S(2)}, u32[]{:S(2)}) %collective-permute-start.27) | collective-permute-done | bytes 73760 | tf_op jit(solution)/shard_map/ppermute | solution.py:62
  81.1 1.6 collective-permute-start.28
  82.7 4.3 %collective-permute-start.29 = (f32[24,768]{1,0:T(8,128)S(1)}, f32[24,768]{1,0:T(8,128)S(1)}, u32[]{:S(2)}, u32[]{:S(2)}) collective-permute-start(f32[24,768]{1,0:T(8,128)S(1)} %step_piece.3.refs_0_), channel_id=1, source_target_pairs={{0,2},{1,3},{2,0},{3,1},{4,6},{5,7},{6,4},{7,5},{8,10},{9,11},{10,... | collective-permute-start | bytes 221192 | tf_op jit(solution)/shard_map/ppermute | solution.py:62
  87.7 2.6 %collective-permute-done.29.refs_2_ = f32[24,768]{1,0:T(8,128)S(1)} collective-permute-done((f32[24,768]{1,0:T(8,128)S(1)}, f32[24,768]{1,0:T(8,128)S(1)}, u32[]{:S(2)}, u32[]{:S(2)}) %collective-permute-start.29) | collective-permute-done | bytes 73760 | tf_op jit(solution)/shard_map/ppermute | solution.py:62
  92.8 2.1 %collective-permute-start.33 = (f32[96,768]{1,0:T(8,128)S(1)}, f32[96,768]{1,0:T(8,128)S(1)}, u32[]{:S(2)}, u32[]{:S(2)}) collective-permute-start(f32[96,768]{1,0:T(8,128)S(1)} %stack.5.refs_0_), channel_id=1, source_target_pairs={{0,24},{1,25},{2,26},{3,27},{4,28},{5,29},{6,30},{7,31},{8,16},{9,... | collective-permute-start | bytes 884744 | tf_op jit(solution)/shard_map/ppermute | solution.py:62
  97.0 13.6 %collective-permute-done.44.refs_2_ = f32[48,768]{1,0:T(8,128)S(1)} collective-permute-done((f32[48,768]{1,0:T(8,128)S(1)}, f32[48,768]{1,0:T(8,128)S(1)}, u32[]{:S(2)}, u32[]{:S(2)}) %collective-permute-start.44) | collective-permute-done | bytes 147488 | tf_op jit(solution)/shard_map/ppermute | solution.py:62
  112.3 2.0 %collective-permute-start.47 = (f32[192,768]{1,0:T(8,128)S(1)}, f32[192,768]{1,0:T(8,128)S(1)}, u32[]{:S(2)}, u32[]{:S(2)}) collective-permute-start(f32[192,768]{1,0:T(8,128)S(1)} %place_rows.1.refs_0_), channel_id=1, source_target_pairs={{0,2},{1,3},{2,0},{3,1},{4,6},{5,7},{6,4},{7,5},{8,10},{9,11},{10,... | collective-permute-start | bytes 1769480 | tf_op jit(solution)/shard_map/ppermute | solution.py:62
  116.9 24.3 %orthogonal.1 = (f32[192,768]{1,0:T(8,128)}, bf16[768,768]{1,0:T(8,128)(2,1)S(1)}, bf16[768,768]{1,0:T(8,128)(2,1)S(1)}) custom-call(f32[96,768]{1,0:T(8,128)S(1)} %stack.5.refs_0_, f32[96,768]{1,0:T(8,128)S(1)} %collective-permute-done.31.refs_1_, f32[96,768]{1,0:T(8,128)S(1)} %collective-permute-done.32.refs_2_, ...), custom_call_target="tpu_custom_call" | custom-call | tf_op jit(solution)/shard_map/orthogonal/pallas_call | solution.py:358
  141.2 12.1 %collective-permute-done.47.refs_2_ = f32[192,768]{1,0:T(8,128)S(1)} collective-permute-done((f32[192,768]{1,0:T(8,128)S(1)}, f32[192,768]{1,0:T(8,128)S(1)}, u32[]{:S(2)}, u32[]{:S(2)}) %collective-permute-start.47) | collective-permute-done | bytes 589856 | tf_op jit(solution)/shard_map/ppermute | solution.py:62
  153.3 12.8 %collective-permute-done.48.refs_3_ = f32[192,768]{1,0:T(8,128)S(1)} collective-permute-done((f32[192,768]{1,0:T(8,128)S(1)}, f32[192,768]{1,0:T(8,128)S(1)}, u32[]{:S(2)}, u32[]{:S(2)}) %collective-permute-start.48) | collective-permute-done | bytes 589856 | tf_op jit(solution)/shard_map/ppermute | solution.py:62
  166.1 3.5 %environment.1 = f32[192,768]{1,0:T(8,128)} custom-call(f32[192,768]{1,0:T(8,128)S(1)} %place_rows.1.refs_0_, f32[192,768]{1,0:T(8,128)S(1)} %collective-permute-done.46.refs_1_, f32[192,768]{1,0:T(8,128)S(1)} %collective-permute-done.47.refs_2_, f32[192,768]{1,0:T(8,128)S(1)} %collective-permute-done.48.refs_3_, ...), custom_call_target="tpu_custom_call" | custom-call | tf_op jit(solution)/shard_map/environment/pallas_call | solution.py:385
  (108 shorter events, 43.3 us)
Async XLA Ops:
  1.5 7.9 %collective-permute-start = (f32[24,768]{1,0:T(8,128)S(1)}, f32[24,768]{1,0:T(8,128)S(1)}, u32[]{:S(2)}, u32[]{:S(2)}) collective-permute-start(f32[24,768]{1,0:T(8,128)S(1)} %constant_dynamic-slice_fusion.base_ref), channel_id=1, source_target_pairs={{0,3},{1,2},{2,1},{3,0},{4,7},{5,6},{6,5},{7,4},{8,11},{9,10},{10,... | collective-permute-start | bytes 221192 | tf_op jit(solution)/shard_map/ppermute | solution.py:62
  10.8 8.4 %collective-permute-start.3 = (f32[72,768]{1,0:T(8,128)S(1)}, f32[72,768]{1,0:T(8,128)S(1)}, u32[]{:S(2)}, u32[]{:S(2)}) collective-permute-start(f32[72,768]{1,0:T(8,128)S(1)} %stack.3.refs_1_), channel_id=1, source_target_pairs={{0,8},{1,9},{2,10},{3,11},{4,12},{5,13},{6,14},{7,15},{8,0},{9,1},... | collective-permute-start | bytes 663560 | tf_op jit(solution)/shard_map/ppermute | solution.py:62
  12.4 10.5 %collective-permute-start.4 = (f32[72,768]{1,0:T(8,128)S(1)}, f32[72,768]{1,0:T(8,128)S(1)}, u32[]{:S(2)}, u32[]{:S(2)}) collective-permute-start(f32[72,768]{1,0:T(8,128)S(1)} %stack.3.refs_1_), channel_id=1, source_target_pairs={{0,16},{1,17},{2,18},{3,19},{4,20},{5,21},{6,22},{7,23},{8,24},{9,... | collective-permute-start | bytes 663560 | tf_op jit(solution)/shard_map/ppermute | solution.py:62
  13.9 9.0 %collective-permute-start.5 = (f32[72,768]{1,0:T(8,128)S(1)}, f32[72,768]{1,0:T(8,128)S(1)}, u32[]{:S(2)}, u32[]{:S(2)}) collective-permute-start(f32[72,768]{1,0:T(8,128)S(1)} %stack.3.refs_1_), channel_id=1, source_target_pairs={{0,24},{1,25},{2,26},{3,27},{4,28},{5,29},{6,30},{7,31},{8,16},{9,... | collective-permute-start | bytes 663560 | tf_op jit(solution)/shard_map/ppermute | solution.py:62
  14.4 9.1 %collective-permute-start.6 = (f32[72,768]{1,0:T(8,128)S(1)}, f32[72,768]{1,0:T(8,128)S(1)}, u32[]{:S(2)}, u32[]{:S(2)}) collective-permute-start(f32[72,768]{1,0:T(8,128)S(1)} %stack.3.refs_1_), channel_id=1, source_target_pairs={{0,4},{1,5},{2,6},{3,7},{4,0},{5,1},{6,2},{7,3},{8,12},{9,13},{10,... | collective-permute-start | bytes 663560 | tf_op jit(solution)/shard_map/ppermute | solution.py:62
  36.8 8.2 %collective-permute-start.14 = (f32[24,768]{1,0:T(8,128)S(1)}, f32[24,768]{1,0:T(8,128)S(1)}, u32[]{:S(2)}, u32[]{:S(2)}) collective-permute-start(f32[24,768]{1,0:T(8,128)S(1)} %get-tuple-element.56.refs_0_), channel_id=1, source_target_pairs={{0,3},{1,2},{2,1},{3,0},{4,7},{5,6},{6,5},{7,4},{8,11},{9,10},{10,... | collective-permute-start | bytes 221192 | tf_op jit(solution)/shard_map/ppermute | solution.py:62
  37.2 7.8 %collective-permute-start.15 = (f32[24,768]{1,0:T(8,128)S(1)}, f32[24,768]{1,0:T(8,128)S(1)}, u32[]{:S(2)}, u32[]{:S(2)}) collective-permute-start(f32[24,768]{1,0:T(8,128)S(1)} %get-tuple-element.56.refs_0_), channel_id=1, source_target_pairs={{0,2},{1,3},{2,0},{3,1},{4,6},{5,7},{6,4},{7,5},{8,10},{9,11},{10,... | collective-permute-start | bytes 221192 | tf_op jit(solution)/shard_map/ppermute | solution.py:62
  45.5 9.9 %collective-permute-start.17 = (f32[96,768]{1,0:T(8,128)S(1)}, f32[96,768]{1,0:T(8,128)S(1)}, u32[]{:S(2)}, u32[]{:S(2)}) collective-permute-start(f32[96,768]{1,0:T(8,128)S(1)} %stack.4.refs_0_), channel_id=1, source_target_pairs={{0,8},{1,9},{2,10},{3,11},{4,12},{5,13},{6,14},{7,15},{8,0},{9,1},... | collective-permute-start | bytes 884744 | tf_op jit(solution)/shard_map/ppermute | solution.py:62
  47.1 12.5 %collective-permute-start.18 = (f32[96,768]{1,0:T(8,128)S(1)}, f32[96,768]{1,0:T(8,128)S(1)}, u32[]{:S(2)}, u32[]{:S(2)}) collective-permute-start(f32[96,768]{1,0:T(8,128)S(1)} %stack.4.refs_0_), channel_id=1, source_target_pairs={{0,16},{1,17},{2,18},{3,19},{4,20},{5,21},{6,22},{7,23},{8,24},{9,... | collective-permute-start | bytes 884744 | tf_op jit(solution)/shard_map/ppermute | solution.py:62
  47.8 11.9 %collective-permute-start.19 = (f32[96,768]{1,0:T(8,128)S(1)}, f32[96,768]{1,0:T(8,128)S(1)}, u32[]{:S(2)}, u32[]{:S(2)}) collective-permute-start(f32[96,768]{1,0:T(8,128)S(1)} %stack.4.refs_0_), channel_id=1, source_target_pairs={{0,24},{1,25},{2,26},{3,27},{4,28},{5,29},{6,30},{7,31},{8,16},{9,... | collective-permute-start | bytes 884744 | tf_op jit(solution)/shard_map/ppermute | solution.py:62
  49.1 11.1 %collective-permute-start.38 = (f32[96,768]{1,0:T(8,128)S(1)}, f32[96,768]{1,0:T(8,128)S(1)}, u32[]{:S(2)}, u32[]{:S(2)}) collective-permute-start(f32[96,768]{1,0:T(8,128)S(1)} %get-tuple-element.65), channel_id=1, source_target_pairs={{0,4},{1,5},{2,6},{3,7},{4,0},{5,1},{6,2},{7,3},{8,12},{9,13},{10,... | collective-permute-start | bytes 884744 | tf_op jit(solution)/shard_map/ppermute | solution.py:62
  49.1 12.0 %collective-permute-start.20 = (f32[96,768]{1,0:T(8,128)S(1)}, f32[96,768]{1,0:T(8,128)S(1)}, u32[]{:S(2)}, u32[]{:S(2)}) collective-permute-start(f32[96,768]{1,0:T(8,128)S(1)} %stack.4.refs_0_), channel_id=1, source_target_pairs={{0,4},{1,5},{2,6},{3,7},{4,0},{5,1},{6,2},{7,3},{8,12},{9,13},{10,... | collective-permute-start | bytes 884744 | tf_op jit(solution)/shard_map/ppermute | solution.py:62
  64.7 8.2 %collective-permute-start.24 = (f32[96,768]{1,0:T(8,128)S(1)}, f32[96,768]{1,0:T(8,128)S(1)}, u32[]{:S(2)}, u32[]{:S(2)}) collective-permute-start(f32[96,768]{1,0:T(8,128)S(1)} %get-tuple-element.58), channel_id=1, source_target_pairs={{0,4},{1,5},{2,6},{3,7},{4,0},{5,1},{6,2},{7,3},{8,12},{9,13},{10,... | collective-permute-start | bytes 884744 | tf_op jit(solution)/shard_map/ppermute | solution.py:62
  72.8 14.1 %collective-permute-start.42 = (f32[96,768]{1,0:T(8,128)S(1)}, f32[96,768]{1,0:T(8,128)S(1)}, u32[]{:S(2)}, u32[]{:S(2)}) collective-permute-start(f32[96,768]{1,0:T(8,128)S(1)} %get-tuple-element.71), channel_id=1, source_target_pairs={{0,4},{1,5},{2,6},{3,7},{4,0},{5,1},{6,2},{7,3},{8,12},{9,13},{10,... | collective-permute-start | bytes 884744 | tf_op jit(solution)/shard_map/ppermute | solution.py:62
  82.7 7.7 %collective-permute-start.29 = (f32[24,768]{1,0:T(8,128)S(1)}, f32[24,768]{1,0:T(8,128)S(1)}, u32[]{:S(2)}, u32[]{:S(2)}) collective-permute-start(f32[24,768]{1,0:T(8,128)S(1)} %step_piece.3.refs_0_), channel_id=1, source_target_pairs={{0,2},{1,3},{2,0},{3,1},{4,6},{5,7},{6,4},{7,5},{8,10},{9,11},{10,... | collective-permute-start | bytes 221192 | tf_op jit(solution)/shard_map/ppermute | solution.py:62
  87.0 8.6 %collective-permute-start.43 = (f32[48,768]{1,0:T(8,128)S(1)}, f32[48,768]{1,0:T(8,128)S(1)}, u32[]{:S(2)}, u32[]{:S(2)}) collective-permute-start(f32[48,768]{1,0:T(8,128)S(1)} %get-tuple-element.73), channel_id=1, source_target_pairs={{0,8},{1,9},{2,10},{3,11},{4,12},{5,13},{6,14},{7,15},{8,0},{9,1},... | collective-permute-start | bytes 442376 | tf_op jit(solution)/shard_map/ppermute | solution.py:62
  91.3 19.4 %collective-permute-start.31 = (f32[96,768]{1,0:T(8,128)S(1)}, f32[96,768]{1,0:T(8,128)S(1)}, u32[]{:S(2)}, u32[]{:S(2)}) collective-permute-start(f32[96,768]{1,0:T(8,128)S(1)} %stack.5.refs_0_), channel_id=1, source_target_pairs={{0,8},{1,9},{2,10},{3,11},{4,12},{5,13},{6,14},{7,15},{8,0},{9,1},... | collective-permute-start | bytes 884744 | tf_op jit(solution)/shard_map/ppermute | solution.py:62
  92.1 20.2 %collective-permute-start.32 = (f32[96,768]{1,0:T(8,128)S(1)}, f32[96,768]{1,0:T(8,128)S(1)}, u32[]{:S(2)}, u32[]{:S(2)}) collective-permute-start(f32[96,768]{1,0:T(8,128)S(1)} %stack.5.refs_0_), channel_id=1, source_target_pairs={{0,16},{1,17},{2,18},{3,19},{4,20},{5,21},{6,22},{7,23},{8,24},{9,... | collective-permute-start | bytes 884744 | tf_op jit(solution)/shard_map/ppermute | solution.py:62
  92.8 21.5 %collective-permute-start.33 = (f32[96,768]{1,0:T(8,128)S(1)}, f32[96,768]{1,0:T(8,128)S(1)}, u32[]{:S(2)}, u32[]{:S(2)}) collective-permute-start(f32[96,768]{1,0:T(8,128)S(1)} %stack.5.refs_0_), channel_id=1, source_target_pairs={{0,24},{1,25},{2,26},{3,27},{4,28},{5,29},{6,30},{7,31},{8,16},{9,... | collective-permute-start | bytes 884744 | tf_op jit(solution)/shard_map/ppermute | solution.py:62
  94.9 15.7 %collective-permute-start.44 = (f32[48,768]{1,0:T(8,128)S(1)}, f32[48,768]{1,0:T(8,128)S(1)}, u32[]{:S(2)}, u32[]{:S(2)}) collective-permute-start(f32[48,768]{1,0:T(8,128)S(1)} %get-tuple-element.74), channel_id=1, source_target_pairs={{0,16},{1,17},{2,18},{3,19},{4,20},{5,21},{6,22},{7,23},{8,24},{9,... | collective-permute-start | bytes 442376 | tf_op jit(solution)/shard_map/ppermute | solution.py:62
  95.6 15.0 %collective-permute-start.45 = (f32[48,768]{1,0:T(8,128)S(1)}, f32[48,768]{1,0:T(8,128)S(1)}, u32[]{:S(2)}, u32[]{:S(2)}) collective-permute-start(f32[48,768]{1,0:T(8,128)S(1)} %get-tuple-element.75), channel_id=1, source_target_pairs={{0,24},{1,25},{2,26},{3,27},{4,28},{5,29},{6,30},{7,31},{8,16},{9,... | collective-permute-start | bytes 442376 | tf_op jit(solution)/shard_map/ppermute | solution.py:62
  111.2 29.9 %collective-permute-start.46 = (f32[192,768]{1,0:T(8,128)S(1)}, f32[192,768]{1,0:T(8,128)S(1)}, u32[]{:S(2)}, u32[]{:S(2)}) collective-permute-start(f32[192,768]{1,0:T(8,128)S(1)} %place_rows.1.refs_0_), channel_id=1, source_target_pairs={{0,1},{1,0},{2,3},{3,2},{4,5},{5,4},{6,7},{7,6},{8,9},{9,8},{10,11... | collective-permute-start | bytes 1769480 | tf_op jit(solution)/shard_map/ppermute | solution.py:62
  112.3 41.0 %collective-permute-start.47 = (f32[192,768]{1,0:T(8,128)S(1)}, f32[192,768]{1,0:T(8,128)S(1)}, u32[]{:S(2)}, u32[]{:S(2)}) collective-permute-start(f32[192,768]{1,0:T(8,128)S(1)} %place_rows.1.refs_0_), channel_id=1, source_target_pairs={{0,2},{1,3},{2,0},{3,1},{4,6},{5,7},{6,4},{7,5},{8,10},{9,11},{10,... | collective-permute-start | bytes 1769480 | tf_op jit(solution)/shard_map/ppermute | solution.py:62
  114.2 51.8 %collective-permute-start.48 = (f32[192,768]{1,0:T(8,128)S(1)}, f32[192,768]{1,0:T(8,128)S(1)}, u32[]{:S(2)}, u32[]{:S(2)}) collective-permute-start(f32[192,768]{1,0:T(8,128)S(1)} %place_rows.1.refs_0_), channel_id=1, source_target_pairs={{0,3},{1,2},{2,1},{3,0},{4,7},{5,6},{6,5},{7,4},{8,11},{9,10},{10,... | collective-permute-start | bytes 1769480 | tf_op jit(solution)/shard_map/ppermute | solution.py:62
  (32 other events, 160.9 us)

commit v2 on v1

--- a/solution.py
+++ b/solution.py
@@ -85,18 +85,19 @@
     )(left)
 
 
-def split_right(right):
-    def kernel(right_ref, rh_ref, rl_ref):
+def split_right(right, amplitudes):
+    def kernel(right_ref, amplitudes_ref, rh_ref, rl_ref, copy_ref):
         rh_ref[...], rl_ref[...] = halves(right_ref[...])
-
-    return pl.pallas_call(
-        kernel,
-        out_shape=(shape(right.shape, BF16),) * 2,
-        in_specs=[VMEM],
-        out_specs=(VMEM,) * 2,
+        copy_ref[...] = amplitudes_ref[...]
+
+    return pl.pallas_call(
+        kernel,
+        out_shape=(shape(right.shape, BF16),) * 2 + (shape(amplitudes.shape),),
+        in_specs=[VMEM] * 2,
+        out_specs=(VMEM,) * 3,
         compiler_params=pltpu.CompilerParams(vmem_limit_bytes=4 * MIB),
         name="split_right",
-    )(right)
+    )(right, amplitudes)
 
 
 def pair_pieces(places, own, received):
@@ -136,6 +137,7 @@
 
 def combine_exchanged(places, parts, source_list, list_count, weight_index, weight_table):
     fan = source_list.shape[1]
+    source_list, weight_index = source_list.T, weight_index.T
     width = parts[0].shape[1]
     piece, half = places.piece, places.half
 
@@ -148,8 +150,8 @@
                 j = (chip ^ slot) * places.cores + (core ^ side)
                 total = None
                 for c in range(fan):
-                    weight = jnp.where(c < count_ref[j], table_ref[index_ref[j, c]], 0.0)
-                    start = pl.multiple_of(source_ref[j, c] * piece, 8)
+                    weight = jnp.where(c < count_ref[j], table_ref[index_ref[c, j]], 0.0)
+                    start = pl.multiple_of(source_ref[c, j] * piece, 8)
                     term = weight * whole[pl.ds(start, piece), :]
                     total = term if total is None else total + term
                 out[pl.ds(slot * piece, piece), :] = total
@@ -183,12 +185,13 @@
 
 def assemble(places, layout, parts, store):
     chip, core, line = places.here()
-    for (chip_slot, core_slot, row_slots, rows_each), part in zip(layout, parts):
-        for index, row_slot in enumerate(row_slots):
-            start = (line ^ row_slot) * places.slab
-            if rows_each != places.slab:
+    for (core_slot, blocks), part in zip(layout, parts):
+        for index, (chip_slot, row_slot) in enumerate(blocks):
+            start, height = (line ^ row_slot) * places.slab, places.slab
+            if chip_slot is not None:
                 start = start + (core ^ core_slot) * places.half + (chip ^ chip_slot) * places.piece
-            store(pl.multiple_of(start, 8), rows_each, part[pl.ds(index * rows_each, rows_each), :])
+                height = places.piece
+            store(pl.multiple_of(start, 8), height, part[pl.ds(index * height, height), :])
 
 
 def put_in(whole):
@@ -282,20 +285,26 @@
 
 
 def spread(places, piece, with_own=True, ready=()):
-    slots = [0] if with_own else []
-    lines = [piece] if with_own else []
-    for slot in reversed(range(1, places.rows)):
-        slots.append(slot)
-        lines.append(places.swap(piece, row=slot))
+    chips = range(1, places.chips)
+    slots = list(reversed(range(1, places.rows)))
+    layout, parts = [], []
+
+    def both_cores(blocks, part):
+        other = places.swap(part, core=1)
+        layout.extend([(0, blocks), (1, blocks)])
+        parts.extend([part, other])
+
+    lines = [places.swap(piece, row=slot) for slot in slots]
+    if with_own:
+        own = [piece] + [places.swap(piece, chip=slot) for slot in chips]
     mine = stack(lines)
     if ready:
         mine, *ready = lax.optimization_barrier((mine, *ready))
-    chips = [mine] + [places.swap(mine, chip=slot) for slot in range(1, places.chips)]
-    layout, parts = [], []
-    for core_slot in range(places.cores):
-        for slot, part in enumerate(chips):
-            layout.append((slot, core_slot, slots, places.piece))
-            parts.append(places.swap(part, core=core_slot) if core_slot else part)
+    gathered = [mine] + [places.swap(mine, chip=slot) for slot in chips]
+    if with_own:
+        both_cores([(slot, 0) for slot in range(places.chips)], stack(own))
+    for chip_slot, part in enumerate(gathered):
+        both_cores([(chip_slot, slot) for slot in slots], part)
     return layout, parts, ready
 
 
@@ -313,14 +322,15 @@
 
     def kernel(*refs):
         count = len(parts)
-        slab_ref, high, low, iterate, gram, poly, gram_high, gram_low, poly_high, poly_low = refs[count:]
+        slab_ref, high, low, iterate, gram, gram_high, gram_low, poly_high, poly_low, *spare = refs[count:]
+        pairs = (spare[:2], spare[2:])
         assemble(places, layout, refs[:count], put_in(gram))
         values = gram[...].T
         values = values * (1.0 / jnp.sqrt(jnp.sum(values * values)))
         iterate[...] = values
-        high[...], low[...] = halves(values)
-
-        def symmetric(out, left, over, finish):
+        spare[0][...], spare[1][...] = halves(values)
+
+        def symmetric(left, over, finish, out_high, out_low):
             for i in range(blocks):
                 rows = pl.ds(i * tile, tile)
                 rest = pl.ds(i * tile, width - i * tile)
@@ -329,27 +339,32 @@
                 else:
                     right = (left[0][:, rest], left[1][:, rest])
                 strip = finish(product((left[0][rows, :], left[1][rows, :]), right, over), rows, rest)
-                out[rows, rest] = strip
+                out_high[rows, rest], out_low[rows, rest] = halves(strip)
                 for j in range(i + 1, blocks):
-                    out[pl.ds(j * tile, tile), rows] = strip[:, (j - i) * tile : (j - i + 1) * tile].T
+                    below = pl.ds(j * tile, tile)
+                    mirrored = strip[:, (j - i) * tile : (j - i + 1) * tile].T
+                    out_high[below, rows], out_low[below, rows] = halves(mirrored)
+
+        def keep_gram(value, rows, rest):
+            gram[rows, rest] = value
+            return value
+
+        def polynomial(value, rows, rest):
+            return COEF_TWO * gram[rows, rest] + COEF_THREE * value
 
         for repeat in range(SWEEPS):
-            symmetric(gram, (high, low), (1, 1), lambda value, rows, rest: value)
-            gram_high[...], gram_low[...] = halves(gram[...])
-            symmetric(
-                poly,
-                (gram_high, gram_low),
-                (1, 0),
-                lambda value, rows, rest: COEF_TWO * gram[rows, rest] + COEF_THREE * value,
-            )
-            poly_high[...], poly_low[...] = halves(poly[...])
-            right = (high[...], low[...])
-            scale = math.sqrt(width) if repeat == SWEEPS - 1 else 1.0
+            here, there = pairs[repeat % 2], pairs[(repeat + 1) % 2]
+            symmetric(here, (1, 1), keep_gram, gram_high, gram_low)
+            symmetric((gram_high, gram_low), (1, 0), polynomial, poly_high, poly_low)
+            last = repeat == SWEEPS - 1
+            scale = math.sqrt(width) if last else 1.0
+            there = (high, low) if last else there
             for i in range(blocks):
                 rows = pl.ds(i * tile, tile)
-                moved = product((poly_high[rows, :], poly_low[rows, :]), right)
-                iterate[rows, :] = scale * (COEF_ONE * iterate[rows, :] + moved)
-            high[...], low[...] = halves(iterate[...])
+                moved = product((poly_high[rows, :], poly_low[rows, :]), (here[0][...], here[1][...]))
+                values = scale * (COEF_ONE * iterate[rows, :] + moved)
+                iterate[rows, :] = values
+                there[0][rows, :], there[1][rows, :] = halves(values)
         gram[...] = iterate[...].T
         line = lax.axis_index("rows")
         slab_ref[...] = gram[pl.ds(pl.multiple_of(line * slab, 8), slab), :]
@@ -360,7 +375,7 @@
         out_shape=(shape((slab, width)),) + (shape(square, BF16),) * 2,
         in_specs=[VMEM] * len(parts),
         out_specs=(VMEM,) * 3,
-        scratch_shapes=[pltpu.VMEM(square, F32)] * 3 + [pltpu.VMEM(square, BF16)] * 4,
+        scratch_shapes=[pltpu.VMEM(square, F32)] * 2 + [pltpu.VMEM(square, BF16)] * 8,
         compiler_params=pltpu.CompilerParams(vmem_limit_bytes=24 * MIB),
         name="orthogonal",
     )(*parts)
@@ -436,20 +451,22 @@
     lists = (source_list, list_count, weight_index, weight_table)
     chip, core, line = places.here()
     every = list(range(rows))
-    slabs = [(0, 0, [slot], slab) for slot in every]
+    slabs = [(0, [(None, slot)]) for slot in every]
     if swappable(terms, rows, slab):
         own, away, *left_halves = order_left(places, left)
-        prepared = (*left_halves, *split_right(right))
+        prepared = (*left_halves, *split_right(right, amplitudes))
         pieces = exchange(places, own, away)
         own, away = combine_exchanged(places, pieces, *lists)
         combined = place_rows(places, exchange(places, own, away))
         start = core * places.half + chip * places.piece
         base = lax.dynamic_slice_in_dim(amplitudes, start, places.piece, 0)
         layout, parts, prepared = spread(places, base, with_own=False, ready=prepared)
+        *prepared, amplitudes = prepared
         layout, parts = [slabs[0]] + layout, [amplitudes] + parts
         for name in ("f", "x"):
             keep, send = apply_terms(places, layout, parts, prepared)
-            sent, *kept = step_piece(base, reduced(places, keep, send), 2 if name == "f" else 1)
+            pieces = reduced(places, keep, send)
+            sent, *kept = step_piece(base, pieces, 2 if name == "f" else 1)
             layout, parts, _ = spread(places, sent)
             base = kept[0] if kept else None
         blocks = [combined]

time: 170 us -> 167 us (0.982)
  waiting for transfers between devices: 84.1 us -> 76.5 us
  starting transfers between devices: 45.2 us -> 51.2 us
    ppermute x49 -> x57, waiting for transfers between devices: 84.1 us -> 76.5 us  [swap(): return lax.ppermute(value, ('terms', 'rows'), pairs)]
    ppermute x49 -> x57, starting transfers between devices: 45.2 us -> 51.2 us  [swap(): return lax.ppermute(value, ('terms', 'rows'), pairs)]
  transfers between devices with their start and end apart: 49 -> 57, of which waited for: 26 -> 28; matrix products, arithmetic and copies ran while one was open for 0% -> 0% of each run, Pallas kernels for 17% -> 17%
where the time goes in v2:
time: 167 us
  waiting for transfers between devices  76.5 us (46%)
  starting transfers between devices  51.2 us (31%)
  Pallas kernels  34.8 us (21%)
  local copies, waits for them, and re-layouts  3.7 us (2%)
    ppermute x57, waiting for transfers between devices, swap(): return lax.ppermute(value, ('terms', 'rows'), pairs)  76.5 us
    ppermute x57, starting transfers between devices, swap(): return lax.ppermute(value, ('terms', 'rows'), pairs)  51.2 us
    pallas_call x1, Pallas kernels, orthogonal(): pl.pallas_call(kernel, out_shape=(shape((slab, width)),) + (shape(square,...  23.5 us
    pallas_call x2, Pallas kernels, apply_terms(): pl.pallas_call(kernel, out_shape=(shape((half, width)),) * 2, in_specs=[V...  6.06 us
    pallas_call x1, Pallas kernels, environment(): pl.pallas_call(kernel, out_shape=shape((slab, width)), in_specs=[VMEM] *...  3.54 us
  transfers between devices with their start and end apart: 57, of which 28 were waited for; matrix products, arithmetic and copies ran while one was open for 0% of the time, Pallas kernels for 17%

profile of v2, /device:TPU:8, one launch (start us, length us, event | category | flops | bytes accessed | tf_op | source)
XLA Modules:
  0.0 167.1 jit_solution(11885678079869526609)
XLA Ops:
  6.9 1.7 copy-done
  14.4 4.8 %collective-permute-done.4.refs_3_ = f32[72,768]{1,0:T(8,128)S(1)} collective-permute-done((f32[72,768]{1,0:T(8,128)S(1)}, f32[72,768]{1,0:T(8,128)S(1)}, u32[]{:S(2)}, u32[]{:S(2)}) %collective-permute-start.4) | collective-permute-done | bytes 221216 | tf_op jit(solution)/shard_map/ppermute | solution.py:62
  19.2 3.7 %collective-permute-done.6.refs_5_ = f32[72,768]{1,0:T(8,128)S(1)} collective-permute-done((f32[72,768]{1,0:T(8,128)S(1)}, f32[72,768]{1,0:T(8,128)S(1)}, u32[]{:S(2)}, u32[]{:S(2)}) %collective-permute-start.6) | collective-permute-done | bytes 221216 | tf_op jit(solution)/shard_map/ppermute | solution.py:62
  24.8 3.0 %apply.2 = (f32[96,768]{1,0:T(8,128)S(1)}, f32[96,768]{1,0:T(8,128)S(1)}) custom-call(f32[192,768]{1,0:T(8,128)S(1)} %get-tuple-element.47.refs_0_, f32[72,768]{1,0:T(8,128)S(1)} %stack.5.refs_1_, f32[72,768]{1,0:T(8,128)S(1)} %collective-permute-done.3.refs_2_, f32[72,768]{1,0:T(8,128)S(1)} %collective-permute-done.4.refs_3_, ...), custom_call_target="tpu_custom_call" | custom-call | tf_op jit(solution)/shard_map/apply/pallas_call | solution.py:217
  34.9 2.0 %collective-permute-done.13.refs_3_ = f32[24,768]{1,0:T(8,128)S(1)} collective-permute-done((f32[24,768]{1,0:T(8,128)S(1)}, f32[24,768]{1,0:T(8,128)S(1)}, u32[]{:S(2)}, u32[]{:S(2)}) %collective-permute-start.13) | collective-permute-done | bytes 73760 | tf_op jit(solution)/shard_map/ppermute | solution.py:62
  37.3 3.9 %collective-permute-start.19 = (f32[24,768]{1,0:T(8,128)S(1)}, f32[24,768]{1,0:T(8,128)S(1)}, u32[]{:S(2)}, u32[]{:S(2)}) collective-permute-start(f32[24,768]{1,0:T(8,128)S(1)} %get-tuple-element.60.refs_0_), channel_id=1, source_target_pairs={{0,2},{1,3},{2,0},{3,1},{4,6},{5,7},{6,4},{7,5},{8,10},{9,11},{10,... | collective-permute-start | bytes 221192 | tf_op jit(solution)/shard_map/ppermute | solution.py:62
  42.7 2.4 %collective-permute-done.18.refs_0_ = f32[24,768]{1,0:T(8,128)S(1)} collective-permute-done((f32[24,768]{1,0:T(8,128)S(1)}, f32[24,768]{1,0:T(8,128)S(1)}, u32[]{:S(2)}, u32[]{:S(2)}) %collective-permute-start.18) | collective-permute-done | bytes 73760 | tf_op jit(solution)/shard_map/ppermute | solution.py:62
  49.5 3.8 %collective-permute-done.15.refs_2_ = f32[24,768]{1,0:T(8,128)S(1)} collective-permute-done((f32[24,768]{1,0:T(8,128)S(1)}, f32[24,768]{1,0:T(8,128)S(1)}, u32[]{:S(2)}, u32[]{:S(2)}) %collective-permute-start.15) | collective-permute-done | bytes 73760 | tf_op jit(solution)/shard_map/ppermute | solution.py:62
  53.3 5.4 %collective-permute-done.16.refs_3_ = f32[24,768]{1,0:T(8,128)S(1)} collective-permute-done((f32[24,768]{1,0:T(8,128)S(1)}, f32[24,768]{1,0:T(8,128)S(1)}, u32[]{:S(2)}, u32[]{:S(2)}) %collective-permute-start.16) | collective-permute-done | bytes 73760 | tf_op jit(solution)/shard_map/ppermute | solution.py:62
  61.9 2.3 %collective-permute-start.49 = (f32[48,768]{1,0:T(8,128)S(1)}, f32[48,768]{1,0:T(8,128)S(1)}, u32[]{:S(2)}, u32[]{:S(2)}) collective-permute-start(f32[48,768]{1,0:T(8,128)S(1)} %get-tuple-element.73), channel_id=1, source_target_pairs={{0,24},{1,25},{2,26},{3,27},{4,28},{5,29},{6,30},{7,31},{8,16},{9,... | collective-permute-start | bytes 442376 | tf_op jit(solution)/shard_map/ppermute | solution.py:62
  64.2 3.0 %apply.3 = (f32[96,768]{1,0:T(8,128)S(1)}, f32[96,768]{1,0:T(8,128)S(1)}) custom-call(f32[96,768]{1,0:T(8,128)S(1)} %stack.6.refs_0_, f32[96,768]{1,0:T(8,128)S(1)} %collective-permute-done.17.refs_1_, f32[72,768]{1,0:T(8,128)S(1)} %stack.7.refs_2_, f32[72,768]{1,0:T(8,128)S(1)} %collective-permute-done.21.refs_3_, ...), custom_call_target="tpu_custom_call" | custom-call | tf_op jit(solution)/shard_map/apply/pallas_call | solution.py:217
  67.4 2.9 %collective-permute-done.48.refs_2_ = f32[48,768]{1,0:T(8,128)S(1)} collective-permute-done((f32[48,768]{1,0:T(8,128)S(1)}, f32[48,768]{1,0:T(8,128)S(1)}, u32[]{:S(2)}, u32[]{:S(2)}) %collective-permute-start.48) | collective-permute-done | bytes 147488 | tf_op jit(solution)/shard_map/ppermute | solution.py:62
  73.1 1.8 %collective-permute-start.31 = (f32[24,768]{1,0:T(8,128)S(1)}, f32[24,768]{1,0:T(8,128)S(1)}, u32[]{:S(2)}, u32[]{:S(2)}) collective-permute-start(f32[24,768]{1,0:T(8,128)S(1)} %get-tuple-element.66), channel_id=1, source_target_pairs={{0,24},{1,25},{2,26},{3,27},{4,28},{5,29},{6,30},{7,31},{8,16},{9,... | collective-permute-start | bytes 221192 | tf_op jit(solution)/shard_map/ppermute | solution.py:62
  76.0 2.4 %collective-permute-done.30.refs_2_ = f32[24,768]{1,0:T(8,128)S(1)} collective-permute-done((f32[24,768]{1,0:T(8,128)S(1)}, f32[24,768]{1,0:T(8,128)S(1)}, u32[]{:S(2)}, u32[]{:S(2)}) %collective-permute-start.30) | collective-permute-done | bytes 73760 | tf_op jit(solution)/shard_map/ppermute | solution.py:62
  82.8 4.4 %collective-permute-start.37 = (f32[24,768]{1,0:T(8,128)S(1)}, f32[24,768]{1,0:T(8,128)S(1)}, u32[]{:S(2)}, u32[]{:S(2)}) collective-permute-start(f32[24,768]{1,0:T(8,128)S(1)} %step_piece.3.refs_0_), channel_id=1, source_target_pairs={{0,2},{1,3},{2,0},{3,1},{4,6},{5,7},{6,4},{7,5},{8,10},{9,11},{10,... | collective-permute-start | bytes 221192 | tf_op jit(solution)/shard_map/ppermute | solution.py:62
  87.7 1.9 %collective-permute-done.37.refs_1_ = f32[24,768]{1,0:T(8,128)S(1)} collective-permute-done((f32[24,768]{1,0:T(8,128)S(1)}, f32[24,768]{1,0:T(8,128)S(1)}, u32[]{:S(2)}, u32[]{:S(2)}) %collective-permute-start.37) | collective-permute-done | bytes 73760 | tf_op jit(solution)/shard_map/ppermute | solution.py:62
  89.6 2.0 %collective-permute-done.38.refs_2_ = f32[24,768]{1,0:T(8,128)S(1)} collective-permute-done((f32[24,768]{1,0:T(8,128)S(1)}, f32[24,768]{1,0:T(8,128)S(1)}, u32[]{:S(2)}, u32[]{:S(2)}) %collective-permute-start.38) | collective-permute-done | bytes 73760 | tf_op jit(solution)/shard_map/ppermute | solution.py:62
  95.8 5.3 %collective-permute-done.32.refs_1_ = f32[24,768]{1,0:T(8,128)S(1)} collective-permute-done((f32[24,768]{1,0:T(8,128)S(1)}, f32[24,768]{1,0:T(8,128)S(1)}, u32[]{:S(2)}, u32[]{:S(2)}) %collective-permute-start.32) | collective-permute-done | bytes 73760 | tf_op jit(solution)/shard_map/ppermute | solution.py:62
  104.1 6.4 %collective-permute-done.34.refs_3_ = f32[24,768]{1,0:T(8,128)S(1)} collective-permute-done((f32[24,768]{1,0:T(8,128)S(1)}, f32[24,768]{1,0:T(8,128)S(1)}, u32[]{:S(2)}, u32[]{:S(2)}) %collective-permute-start.34) | collective-permute-done | bytes 73760 | tf_op jit(solution)/shard_map/ppermute | solution.py:62
  111.4 2.6 %collective-permute-start.56 = (f32[192,768]{1,0:T(8,128)S(1)}, f32[192,768]{1,0:T(8,128)S(1)}, u32[]{:S(2)}, u32[]{:S(2)}) collective-permute-start(f32[192,768]{1,0:T(8,128)S(1)} %place_rows.1.refs_0_), channel_id=1, source_target_pairs={{0,3},{1,2},{2,1},{3,0},{4,7},{5,6},{6,5},{7,4},{8,11},{9,10},{10,... | collective-permute-start | bytes 1769480 | tf_op jit(solution)/shard_map/ppermute | solution.py:62
  117.4 23.5 %orthogonal.1 = (f32[192,768]{1,0:T(8,128)}, bf16[768,768]{1,0:T(8,128)(2,1)S(1)}, bf16[768,768]{1,0:T(8,128)(2,1)S(1)}) custom-call(f32[96,768]{1,0:T(8,128)S(1)} %stack.8.refs_0_, f32[96,768]{1,0:T(8,128)S(1)} %collective-permute-done.35.refs_1_, f32[72,768]{1,0:T(8,128)S(1)} %stack.9.refs_2_, f32[72,768]{1,0:T(8,128)S(1)} %collective-permute-done.39.refs_3_, ...), custom_call_target="tpu_custom_call" | custom-call | tf_op jit(solution)/shard_map/orthogonal/pallas_call | solution.py:373
  140.9 9.4 %collective-permute-done.55.refs_2_ = f32[192,768]{1,0:T(8,128)S(1)} collective-permute-done((f32[192,768]{1,0:T(8,128)S(1)}, f32[192,768]{1,0:T(8,128)S(1)}, u32[]{:S(2)}, u32[]{:S(2)}) %collective-permute-start.55) | collective-permute-done | bytes 589856 | tf_op jit(solution)/shard_map/ppermute | solution.py:62
  150.4 13.2 %collective-permute-done.56.refs_3_ = f32[192,768]{1,0:T(8,128)S(1)} collective-permute-done((f32[192,768]{1,0:T(8,128)S(1)}, f32[192,768]{1,0:T(8,128)S(1)}, u32[]{:S(2)}, u32[]{:S(2)}) %collective-permute-start.56) | collective-permute-done | bytes 589856 | tf_op jit(solution)/shard_map/ppermute | solution.py:62
  163.6 3.5 %environment.1 = f32[192,768]{1,0:T(8,128)} custom-call(f32[192,768]{1,0:T(8,128)S(1)} %place_rows.1.refs_0_, f32[192,768]{1,0:T(8,128)S(1)} %collective-permute-done.54.refs_1_, f32[192,768]{1,0:T(8,128)S(1)} %collective-permute-done.55.refs_2_, f32[192,768]{1,0:T(8,128)S(1)} %collective-permute-done.56.refs_3_, ...), custom_call_target="tpu_custom_call" | custom-call | tf_op jit(solution)/shard_map/environment/pallas_call | solution.py:400
  (124 shorter events, 50.9 us)
Async XLA Ops:
  10.9 8.4 %collective-permute-start.4 = (f32[72,768]{1,0:T(8,128)S(1)}, f32[72,768]{1,0:T(8,128)S(1)}, u32[]{:S(2)}, u32[]{:S(2)}) collective-permute-start(f32[72,768]{1,0:T(8,128)S(1)} %stack.5.refs_1_), channel_id=1, source_target_pairs={{0,8},{1,9},{2,10},{3,11},{4,12},{5,13},{6,14},{7,15},{8,0},{9,1},... | collective-permute-start | bytes 663560 | tf_op jit(solution)/shard_map/ppermute | solution.py:62
  12.4 10.5 %collective-permute-start.6 = (f32[72,768]{1,0:T(8,128)S(1)}, f32[72,768]{1,0:T(8,128)S(1)}, u32[]{:S(2)}, u32[]{:S(2)}) collective-permute-start(f32[72,768]{1,0:T(8,128)S(1)} %stack.5.refs_1_), channel_id=1, source_target_pairs={{0,16},{1,17},{2,18},{3,19},{4,20},{5,21},{6,22},{7,23},{8,24},{9,... | collective-permute-start | bytes 663560 | tf_op jit(solution)/shard_map/ppermute | solution.py:62
  13.9 9.0 %collective-permute-start.8 = (f32[72,768]{1,0:T(8,128)S(1)}, f32[72,768]{1,0:T(8,128)S(1)}, u32[]{:S(2)}, u32[]{:S(2)}) collective-permute-start(f32[72,768]{1,0:T(8,128)S(1)} %stack.5.refs_1_), channel_id=1, source_target_pairs={{0,24},{1,25},{2,26},{3,27},{4,28},{5,29},{6,30},{7,31},{8,16},{9,... | collective-permute-start | bytes 663560 | tf_op jit(solution)/shard_map/ppermute | solution.py:62
  14.4 9.1 %collective-permute-start.3 = (f32[72,768]{1,0:T(8,128)S(1)}, f32[72,768]{1,0:T(8,128)S(1)}, u32[]{:S(2)}, u32[]{:S(2)}) collective-permute-start(f32[72,768]{1,0:T(8,128)S(1)} %stack.5.refs_1_), channel_id=1, source_target_pairs={{0,4},{1,5},{2,6},{3,7},{4,0},{5,1},{6,2},{7,3},{8,12},{9,13},{10,... | collective-permute-start | bytes 663560 | tf_op jit(solution)/shard_map/ppermute | solution.py:62
  33.0 25.7 %collective-permute-start.46 = (f32[96,768]{1,0:T(8,128)S(1)}, f32[96,768]{1,0:T(8,128)S(1)}, u32[]{:S(2)}, u32[]{:S(2)}) collective-permute-start(f32[96,768]{1,0:T(8,128)S(1)} %get-tuple-element.69), channel_id=1, source_target_pairs={{0,4},{1,5},{2,6},{3,7},{4,0},{5,1},{6,2},{7,3},{8,12},{9,13},{10,... | collective-permute-start | bytes 884744 | tf_op jit(solution)/shard_map/ppermute | solution.py:62
  36.9 8.2 %collective-permute-start.18 = (f32[24,768]{1,0:T(8,128)S(1)}, f32[24,768]{1,0:T(8,128)S(1)}, u32[]{:S(2)}, u32[]{:S(2)}) collective-permute-start(f32[24,768]{1,0:T(8,128)S(1)} %get-tuple-element.60.refs_0_), channel_id=1, source_target_pairs={{0,3},{1,2},{2,1},{3,0},{4,7},{5,6},{6,5},{7,4},{8,11},{9,10},{10,... | collective-permute-start | bytes 221192 | tf_op jit(solution)/shard_map/ppermute | solution.py:62
  37.3 8.6 %collective-permute-start.19 = (f32[24,768]{1,0:T(8,128)S(1)}, f32[24,768]{1,0:T(8,128)S(1)}, u32[]{:S(2)}, u32[]{:S(2)}) collective-permute-start(f32[24,768]{1,0:T(8,128)S(1)} %get-tuple-element.60.refs_0_), channel_id=1, source_target_pairs={{0,2},{1,3},{2,0},{3,1},{4,6},{5,7},{6,4},{7,5},{8,10},{9,11},{10,... | collective-permute-start | bytes 221192 | tf_op jit(solution)/shard_map/ppermute | solution.py:62
  45.1 8.2 %collective-permute-start.15 = (f32[24,768]{1,0:T(8,128)S(1)}, f32[24,768]{1,0:T(8,128)S(1)}, u32[]{:S(2)}, u32[]{:S(2)}) collective-permute-start(f32[24,768]{1,0:T(8,128)S(1)} %get-tuple-element.60.refs_0_), channel_id=1, source_target_pairs={{0,16},{1,17},{2,18},{3,19},{4,20},{5,21},{6,22},{7,23},{8,24},{9,... | collective-permute-start | bytes 221192 | tf_op jit(solution)/shard_map/ppermute | solution.py:62
  45.9 13.3 %collective-permute-start.22 = (f32[72,768]{1,0:T(8,128)S(1)}, f32[72,768]{1,0:T(8,128)S(1)}, u32[]{:S(2)}, u32[]{:S(2)}) collective-permute-start(f32[72,768]{1,0:T(8,128)S(1)} %stack.7.refs_2_), channel_id=1, source_target_pairs={{0,8},{1,9},{2,10},{3,11},{4,12},{5,13},{6,14},{7,15},{8,0},{9,1},... | collective-permute-start | bytes 663560 | tf_op jit(solution)/shard_map/ppermute | solution.py:62
  47.2 12.2 %collective-permute-start.24 = (f32[72,768]{1,0:T(8,128)S(1)}, f32[72,768]{1,0:T(8,128)S(1)}, u32[]{:S(2)}, u32[]{:S(2)}) collective-permute-start(f32[72,768]{1,0:T(8,128)S(1)} %stack.7.refs_2_), channel_id=1, source_target_pairs={{0,16},{1,17},{2,18},{3,19},{4,20},{5,21},{6,22},{7,23},{8,24},{9,... | collective-permute-start | bytes 663560 | tf_op jit(solution)/shard_map/ppermute | solution.py:62
  48.6 11.2 %collective-permute-start.26 = (f32[72,768]{1,0:T(8,128)S(1)}, f32[72,768]{1,0:T(8,128)S(1)}, u32[]{:S(2)}, u32[]{:S(2)}) collective-permute-start(f32[72,768]{1,0:T(8,128)S(1)} %stack.7.refs_2_), channel_id=1, source_target_pairs={{0,24},{1,25},{2,26},{3,27},{4,28},{5,29},{6,30},{7,31},{8,16},{9,... | collective-permute-start | bytes 663560 | tf_op jit(solution)/shard_map/ppermute | solution.py:62
  61.5 8.8 %collective-permute-start.48 = (f32[48,768]{1,0:T(8,128)S(1)}, f32[48,768]{1,0:T(8,128)S(1)}, u32[]{:S(2)}, u32[]{:S(2)}) collective-permute-start(f32[48,768]{1,0:T(8,128)S(1)} %get-tuple-element.72), channel_id=1, source_target_pairs={{0,16},{1,17},{2,18},{3,19},{4,20},{5,21},{6,22},{7,23},{8,24},{9,... | collective-permute-start | bytes 442376 | tf_op jit(solution)/shard_map/ppermute | solution.py:62
  61.9 8.4 %collective-permute-start.49 = (f32[48,768]{1,0:T(8,128)S(1)}, f32[48,768]{1,0:T(8,128)S(1)}, u32[]{:S(2)}, u32[]{:S(2)}) collective-permute-start(f32[48,768]{1,0:T(8,128)S(1)} %get-tuple-element.73), channel_id=1, source_target_pairs={{0,24},{1,25},{2,26},{3,27},{4,28},{5,29},{6,30},{7,31},{8,16},{9,... | collective-permute-start | bytes 442376 | tf_op jit(solution)/shard_map/ppermute | solution.py:62
  78.5 8.7 %collective-permute-start.36 = (f32[24,768]{1,0:T(8,128)S(1)}, f32[24,768]{1,0:T(8,128)S(1)}, u32[]{:S(2)}, u32[]{:S(2)}) collective-permute-start(f32[24,768]{1,0:T(8,128)S(1)} %step_piece.3.refs_0_), channel_id=1, source_target_pairs={{0,3},{1,2},{2,1},{3,0},{4,7},{5,6},{6,5},{7,4},{8,11},{9,10},{10,... | collective-permute-start | bytes 221192 | tf_op jit(solution)/shard_map/ppermute | solution.py:62
  79.3 13.7 %collective-permute-start.51 = (f32[48,768]{1,0:T(8,128)S(1)}, f32[48,768]{1,0:T(8,128)S(1)}, u32[]{:S(2)}, u32[]{:S(2)}) collective-permute-start(f32[48,768]{1,0:T(8,128)S(1)} %get-tuple-element.77), channel_id=1, source_target_pairs={{0,8},{1,9},{2,10},{3,11},{4,12},{5,13},{6,14},{7,15},{8,0},{9,1},... | collective-permute-start | bytes 442376 | tf_op jit(solution)/shard_map/ppermute | solution.py:62
  80.7 13.0 %collective-permute-start.52 = (f32[48,768]{1,0:T(8,128)S(1)}, f32[48,768]{1,0:T(8,128)S(1)}, u32[]{:S(2)}, u32[]{:S(2)}) collective-permute-start(f32[48,768]{1,0:T(8,128)S(1)} %get-tuple-element.78), channel_id=1, source_target_pairs={{0,16},{1,17},{2,18},{3,19},{4,20},{5,21},{6,22},{7,23},{8,24},{9,... | collective-permute-start | bytes 442376 | tf_op jit(solution)/shard_map/ppermute | solution.py:62
  81.4 13.3 %collective-permute-start.53 = (f32[48,768]{1,0:T(8,128)S(1)}, f32[48,768]{1,0:T(8,128)S(1)}, u32[]{:S(2)}, u32[]{:S(2)}) collective-permute-start(f32[48,768]{1,0:T(8,128)S(1)} %get-tuple-element.79), channel_id=1, source_target_pairs={{0,24},{1,25},{2,26},{3,27},{4,28},{5,29},{6,30},{7,31},{8,16},{9,... | collective-permute-start | bytes 442376 | tf_op jit(solution)/shard_map/ppermute | solution.py:62
  91.6 19.4 %collective-permute-start.39 = (f32[72,768]{1,0:T(8,128)S(1)}, f32[72,768]{1,0:T(8,128)S(1)}, u32[]{:S(2)}, u32[]{:S(2)}) collective-permute-start(f32[72,768]{1,0:T(8,128)S(1)} %stack.9.refs_2_), channel_id=1, source_target_pairs={{0,4},{1,5},{2,6},{3,7},{4,0},{5,1},{6,2},{7,3},{8,12},{9,13},{10,... | collective-permute-start | bytes 663560 | tf_op jit(solution)/shard_map/ppermute | solution.py:62
  91.7 19.7 %collective-permute-start.40 = (f32[72,768]{1,0:T(8,128)S(1)}, f32[72,768]{1,0:T(8,128)S(1)}, u32[]{:S(2)}, u32[]{:S(2)}) collective-permute-start(f32[72,768]{1,0:T(8,128)S(1)} %stack.9.refs_2_), channel_id=1, source_target_pairs={{0,8},{1,9},{2,10},{3,11},{4,12},{5,13},{6,14},{7,15},{8,0},{9,1},... | collective-permute-start | bytes 663560 | tf_op jit(solution)/shard_map/ppermute | solution.py:62
  93.0 21.0 %collective-permute-start.42 = (f32[72,768]{1,0:T(8,128)S(1)}, f32[72,768]{1,0:T(8,128)S(1)}, u32[]{:S(2)}, u32[]{:S(2)}) collective-permute-start(f32[72,768]{1,0:T(8,128)S(1)} %stack.9.refs_2_), channel_id=1, source_target_pairs={{0,16},{1,17},{2,18},{3,19},{4,20},{5,21},{6,22},{7,23},{8,24},{9,... | collective-permute-start | bytes 663560 | tf_op jit(solution)/shard_map/ppermute | solution.py:62
  101.1 13.0 %collective-permute-start.44 = (f32[72,768]{1,0:T(8,128)S(1)}, f32[72,768]{1,0:T(8,128)S(1)}, u32[]{:S(2)}, u32[]{:S(2)}) collective-permute-start(f32[72,768]{1,0:T(8,128)S(1)} %stack.9.refs_2_), channel_id=1, source_target_pairs={{0,24},{1,25},{2,26},{3,27},{4,28},{5,29},{6,30},{7,31},{8,16},{9,... | collective-permute-start | bytes 663560 | tf_op jit(solution)/shard_map/ppermute | solution.py:62
  110.5 30.5 %collective-permute-start.54 = (f32[192,768]{1,0:T(8,128)S(1)}, f32[192,768]{1,0:T(8,128)S(1)}, u32[]{:S(2)}, u32[]{:S(2)}) collective-permute-start(f32[192,768]{1,0:T(8,128)S(1)} %place_rows.1.refs_0_), channel_id=1, source_target_pairs={{0,1},{1,0},{2,3},{3,2},{4,5},{5,4},{6,7},{7,6},{8,9},{9,8},{10,11... | collective-permute-start | bytes 1769480 | tf_op jit(solution)/shard_map/ppermute | solution.py:62
  111.0 39.4 %collective-permute-start.55 = (f32[192,768]{1,0:T(8,128)S(1)}, f32[192,768]{1,0:T(8,128)S(1)}, u32[]{:S(2)}, u32[]{:S(2)}) collective-permute-start(f32[192,768]{1,0:T(8,128)S(1)} %place_rows.1.refs_0_), channel_id=1, source_target_pairs={{0,2},{1,3},{2,0},{3,1},{4,6},{5,7},{6,4},{7,5},{8,10},{9,11},{10,... | collective-permute-start | bytes 1769480 | tf_op jit(solution)/shard_map/ppermute | solution.py:62
  111.4 52.2 %collective-permute-start.56 = (f32[192,768]{1,0:T(8,128)S(1)}, f32[192,768]{1,0:T(8,128)S(1)}, u32[]{:S(2)}, u32[]{:S(2)}) collective-permute-start(f32[192,768]{1,0:T(8,128)S(1)} %place_rows.1.refs_0_), channel_id=1, source_target_pairs={{0,3},{1,2},{2,1},{3,0},{4,7},{5,6},{6,5},{7,4},{8,11},{9,10},{10,... | collective-permute-start | bytes 1769480 | tf_op jit(solution)/shard_map/ppermute | solution.py:62
  (40 other events, 196.7 us)

commit v3 on v2

--- a/solution.py
+++ b/solution.py
@@ -34,7 +34,9 @@
 def product(left, right, over=(1, 0)):
     dims = (((over[0],), (over[1],)), ((), ()))
     dot = functools.partial(lax.dot_general, dimension_numbers=dims, preferred_element_type=F32)
-    return dot(left[0], right[0]) + (dot(left[0], right[1]) + dot(left[1], right[0]))
+    count = left[0].shape[0]
+    both = dot(jnp.concatenate(left, axis=0), right[0])
+    return both[:count] + (both[count:] + dot(left[0], right[1]))
 
 
 def shape(dims, dtype=F32):
@@ -85,16 +87,20 @@
     )(left)
 
 
-def split_right(right, amplitudes):
-    def kernel(right_ref, amplitudes_ref, rh_ref, rl_ref, copy_ref):
+def split_right(places, right, amplitudes):
+    def kernel(right_ref, amplitudes_ref, rh_ref, rl_ref, copy_ref, base_ref):
         rh_ref[...], rl_ref[...] = halves(right_ref[...])
         copy_ref[...] = amplitudes_ref[...]
-
-    return pl.pallas_call(
-        kernel,
-        out_shape=(shape(right.shape, BF16),) * 2 + (shape(amplitudes.shape),),
+        chip, core, _ = places.here()
+        start = pl.multiple_of(core * places.half + chip * places.piece, 8)
+        base_ref[...] = amplitudes_ref[pl.ds(start, places.piece), :]
+
+    return pl.pallas_call(
+        kernel,
+        out_shape=(shape(right.shape, BF16),) * 2
+        + (shape(amplitudes.shape), shape((places.piece, right.shape[1]))),
         in_specs=[VMEM] * 2,
-        out_specs=(VMEM,) * 3,
+        out_specs=(VMEM,) * 4,
         compiler_params=pltpu.CompilerParams(vmem_limit_bytes=4 * MIB),
         name="split_right",
     )(right, amplitudes)
@@ -186,12 +192,11 @@
 def assemble(places, layout, parts, store):
     chip, core, line = places.here()
     for (core_slot, blocks), part in zip(layout, parts):
-        for index, (chip_slot, row_slot) in enumerate(blocks):
-            start, height = (line ^ row_slot) * places.slab, places.slab
-            if chip_slot is not None:
-                start = start + (core ^ core_slot) * places.half + (chip ^ chip_slot) * places.piece
-                height = places.piece
-            store(pl.multiple_of(start, 8), height, part[pl.ds(index * height, height), :])
+        first = 0
+        for row_slot, height, place in blocks:
+            start = (line ^ row_slot) * places.slab + place(chip, core ^ core_slot)
+            store(pl.multiple_of(start, 8), height, part[pl.ds(first, height), :])
+            first += height
 
 
 def put_in(whole):
@@ -284,28 +289,75 @@
     )(*parts)
 
 
-def spread(places, piece, with_own=True, ready=()):
+def to_both_cores(places, layout, parts, blocks, part):
+    other = places.swap(part, core=1)
+    layout.extend([(0, blocks), (1, blocks)])
+    parts.extend([part, other])
+
+
+def spread(places, piece):
     chips = range(1, places.chips)
     slots = list(reversed(range(1, places.rows)))
     layout, parts = [], []
 
-    def both_cores(blocks, part):
-        other = places.swap(part, core=1)
-        layout.extend([(0, blocks), (1, blocks)])
-        parts.extend([part, other])
+    def blocks(pairs):
+        def place(slot):
+            return lambda chip, core: core * places.half + (chip ^ slot) * places.piece
+
+        return [(row_slot, places.piece, place(chip_slot)) for chip_slot, row_slot in pairs]
 
     lines = [places.swap(piece, row=slot) for slot in slots]
-    if with_own:
-        own = [piece] + [places.swap(piece, chip=slot) for slot in chips]
+    own = [piece] + [places.swap(piece, chip=slot) for slot in chips]
     mine = stack(lines)
-    if ready:
-        mine, *ready = lax.optimization_barrier((mine, *ready))
     gathered = [mine] + [places.swap(mine, chip=slot) for slot in chips]
-    if with_own:
-        both_cores([(slot, 0) for slot in range(places.chips)], stack(own))
+    own = stack(own)
+    to_both_cores(places, layout, parts, blocks([(slot, 0) for slot in range(places.chips)]), own)
     for chip_slot, part in enumerate(gathered):
-        both_cores([(chip_slot, slot) for slot in slots], part)
+        to_both_cores(places, layout, parts, blocks([(chip_slot, slot) for slot in slots]), part)
+    return layout, parts
+
+
+def spread_slabs(places, slab, ready):
+    part_rows, piece = 2 * places.piece, places.piece
+    slots = list(reversed(range(1, places.rows)))
+    chip, core, _ = places.here()
+
+    def parity(chip):
+        return (chip & 1) ^ (chip >> 1)
+
+    def place(turn, extra):
+        return lambda chip, core: core * places.half + (parity(chip) ^ turn) * part_rows + extra
+
+    start = core * places.half + parity(chip) * part_rows
+    sent = lax.dynamic_slice_in_dim(slab, start, part_rows, 0)
+    lines = [places.swap(sent, row=slot) for slot in slots]
+    firsts, rests = stack_halves(lines)
+    firsts, rests, *ready = lax.optimization_barrier((firsts, rests, *ready))
+    layout, parts = [], []
+    others = [places.swap(firsts, chip=1), places.swap(rests, chip=2)]
+    for turn, extra, part in ((0, 0, firsts), (0, piece, rests), (1, 0, others[0]), (1, piece, others[1])):
+        blocks = [(slot, piece, place(turn, extra)) for slot in slots]
+        to_both_cores(places, layout, parts, blocks, part)
     return layout, parts, ready
+
+
+def stack_halves(parts):
+    width = parts[0].shape[1]
+    height = parts[0].shape[0] // 2
+
+    def kernel(*refs):
+        for side, out in enumerate(refs[-2:]):
+            for index, ref in enumerate(refs[:-2]):
+                out[pl.ds(index * height, height), :] = ref[pl.ds(side * height, height), :]
+
+    return pl.pallas_call(
+        kernel,
+        out_shape=(shape((height * len(parts), width)),) * 2,
+        in_specs=[VMEM] * len(parts),
+        out_specs=(VMEM,) * 2,
+        compiler_params=pltpu.CompilerParams(vmem_limit_bytes=2 * MIB),
+        name="stack_halves",
+    )(*parts)
 
 
 def reduced(places, keep, send):
@@ -322,11 +374,15 @@
 
     def kernel(*refs):
         count = len(parts)
-        slab_ref, high, low, iterate, gram, gram_high, gram_low, poly_high, poly_low, *spare = refs[count:]
+        slab_ref, high, low, mine_high, mine_low = refs[count : count + 5]
+        iterate, gram, gram_high, gram_low, poly_high, poly_low, *spare = refs[count + 5 :]
         pairs = (spare[:2], spare[2:])
         assemble(places, layout, refs[:count], put_in(gram))
-        values = gram[...].T
-        values = values * (1.0 / jnp.sqrt(jnp.sum(values * values)))
+        squares = jnp.zeros((8, width), F32)
+        for i in range(width // 8):
+            some = gram[pl.ds(8 * i, 8), :]
+            squares = squares + some * some
+        values = gram[...].T * (1.0 / jnp.sqrt(jnp.sum(squares)))
         iterate[...] = values
         spare[0][...], spare[1][...] = halves(values)
 
@@ -356,56 +412,59 @@
             here, there = pairs[repeat % 2], pairs[(repeat + 1) % 2]
             symmetric(here, (1, 1), keep_gram, gram_high, gram_low)
             symmetric((gram_high, gram_low), (1, 0), polynomial, poly_high, poly_low)
-            last = repeat == SWEEPS - 1
-            scale = math.sqrt(width) if last else 1.0
-            there = (high, low) if last else there
             for i in range(blocks):
                 rows = pl.ds(i * tile, tile)
                 moved = product((poly_high[rows, :], poly_low[rows, :]), (here[0][...], here[1][...]))
-                values = scale * (COEF_ONE * iterate[rows, :] + moved)
-                iterate[rows, :] = values
-                there[0][rows, :], there[1][rows, :] = halves(values)
-        gram[...] = iterate[...].T
-        line = lax.axis_index("rows")
-        slab_ref[...] = gram[pl.ds(pl.multiple_of(line * slab, 8), slab), :]
+                values = COEF_ONE * iterate[rows, :] + moved
+                if repeat < SWEEPS - 1:
+                    iterate[rows, :] = values
+                    there[0][rows, :], there[1][rows, :] = halves(values)
+                else:
+                    values = math.sqrt(width) * values
+                    iterate[rows, :] = values
+                    upright = values.T
+                    gram[:, rows] = upright
+                    high[:, rows], low[:, rows] = halves(upright)
+        mine = pl.ds(pl.multiple_of(lax.axis_index("rows") * slab, 8), slab)
+        slab_ref[...] = gram[mine, :]
+        mine_high[...], mine_low[...] = halves(iterate[mine, :])
 
     square = (width, width)
     return pl.pallas_call(
         kernel,
-        out_shape=(shape((slab, width)),) + (shape(square, BF16),) * 2,
+        out_shape=(shape((slab, width)),) + (shape(square, BF16),) * 2 + (shape((slab, width), BF16),) * 2,
         in_specs=[VMEM] * len(parts),
-        out_specs=(VMEM,) * 3,
+        out_specs=(VMEM,) * 5,
         scratch_shapes=[pltpu.VMEM(square, F32)] * 2 + [pltpu.VMEM(square, BF16)] * 8,
         compiler_params=pltpu.CompilerParams(vmem_limit_bytes=24 * MIB),
         name="orthogonal",
     )(*parts)
 
 
-def environment(places, layout, parts, high, low):
+def environment(places, layout, parts, high, low, mine_high, mine_low):
     width = high.shape[0]
     slab = places.slab
 
     def kernel(*refs):
         count = len(parts)
-        high_ref, low_ref, out_ref, block_high, block_low = refs[count:]
+        high_ref, low_ref, mh_ref, ml_ref, out_ref, block_high, block_low = refs[count:]
 
         def store(start, height, value):
             block_high[pl.ds(start, height), :], block_low[pl.ds(start, height), :] = halves(value)
 
         assemble(places, layout, refs[:count], store)
-        rows = pl.ds(pl.multiple_of(lax.axis_index("rows") * slab, 16), slab)
-        rotated = product((high_ref[rows, :], low_ref[rows, :]), (block_high[...], block_low[...]))
-        out_ref[...] = product(halves(rotated), (high_ref[...], low_ref[...]), (1, 1))
+        rotated = product((mh_ref[...], ml_ref[...]), (block_high[...], block_low[...]))
+        out_ref[...] = product(halves(rotated), (high_ref[...], low_ref[...]))
 
     return pl.pallas_call(
         kernel,
         out_shape=shape((slab, width)),
-        in_specs=[VMEM] * (len(parts) + 2),
+        in_specs=[VMEM] * (len(parts) + 4),
         out_specs=VMEM,
         scratch_shapes=[pltpu.VMEM((width, width), BF16)] * 2,
         compiler_params=pltpu.CompilerParams(vmem_limit_bytes=10 * MIB),
         name="environment",
-    )(*parts, high, low)
+    )(*parts, high, low, mine_high, mine_low)
 
 
 def combine_pieces(pieces, source_list, list_count, weight_index, weight_table):
@@ -449,25 +508,23 @@
     places = Places(terms, rows, slab)
 
     lists = (source_list, list_count, weight_index, weight_table)
-    chip, core, line = places.here()
+    _, _, line = places.here()
     every = list(range(rows))
-    slabs = [(0, [(None, slot)]) for slot in every]
+    slabs = [(0, [(slot, slab, lambda chip, core: 0)]) for slot in every]
     if swappable(terms, rows, slab):
         own, away, *left_halves = order_left(places, left)
-        prepared = (*left_halves, *split_right(right, amplitudes))
+        prepared = (*left_halves, *split_right(places, right, amplitudes))
         pieces = exchange(places, own, away)
         own, away = combine_exchanged(places, pieces, *lists)
         combined = place_rows(places, exchange(places, own, away))
-        start = core * places.half + chip * places.piece
-        base = lax.dynamic_slice_in_dim(amplitudes, start, places.piece, 0)
-        layout, parts, prepared = spread(places, base, with_own=False, ready=prepared)
-        *prepared, amplitudes = prepared
+        layout, parts, prepared = spread_slabs(places, amplitudes, prepared)
+        *prepared, amplitudes, base = prepared
         layout, parts = [slabs[0]] + layout, [amplitudes] + parts
         for name in ("f", "x"):
             keep, send = apply_terms(places, layout, parts, prepared)
             pieces = reduced(places, keep, send)
             sent, *kept = step_piece(base, pieces, 2 if name == "f" else 1)
-            layout, parts, _ = spread(places, sent)
+            layout, parts = spread(places, sent)
             base = kept[0] if kept else None
         blocks = [combined]
         for slot in every[1:]:
@@ -485,13 +542,13 @@
         combined = combined_slab(left, *lists)
         full = lax.all_gather(combined, "rows", axis=0, tiled=True)
         blocks = [lax.dynamic_slice_in_dim(full, (line ^ slot) * slab, slab, 0) for slot in every]
-    isometry, high, low = orthogonal(places, layout, parts)
-    new_environment = environment(places, slabs, blocks, high, low)
+    isometry, *turned = orthogonal(places, layout, parts)
+    new_environment = environment(places, slabs, blocks, *turned)
     return (isometry, new_environment[None])
 
 
 def swappable(terms, rows, slab):
-    return terms <= 8 and terms & (terms - 1) == 0 and rows & (rows - 1) == 0 and slab % (8 * terms) == 0
+    return terms == 8 and rows & (rows - 1) == 0 and slab % (8 * terms) == 0
 
 
 def solution(mesh):

time: 167 us -> 165 us (0.988)
  Pallas kernels: 34.8 us -> 30.8 us
    pallas_call x2, Pallas kernels: 6.06 us -> 4.15 us  [apply_terms(): pl.pallas_call(kernel, out_shape=(shape((half, width)),) * 2, in_specs=[V...]
    pallas_call x1, Pallas kernels: 23.5 us -> 21.7 us  [orthogonal(): pl.pallas_call(kernel, out_shape=(shape((slab, width)),) + (shape(square,...]
    ppermute x57 -> x56, waiting for transfers between devices: 76.5 us -> 77.5 us  [swap(): return lax.ppermute(value, ('terms', 'rows'), pairs)]
    ppermute x57 -> x56, starting transfers between devices: 51.2 us -> 51.9 us  [swap(): return lax.ppermute(value, ('terms', 'rows'), pairs)]
  transfers between devices with their start and end apart: 57 -> 56, of which waited for: 28 -> 30; matrix products, arithmetic and copies ran while one was open for 0% -> 0% of each run, Pallas kernels for 17% -> 15%
where the time goes in v3:
time: 165 us
  waiting for transfers between devices  77.5 us (47%)
  starting transfers between devices  51.9 us (31%)
  Pallas kernels  30.8 us (19%)
  local copies, waits for them, and re-layouts  3.73 us (2%)
    ppermute x56, waiting for transfers between devices, swap(): return lax.ppermute(value, ('terms', 'rows'), pairs)  77.5 us
    ppermute x56, starting transfers between devices, swap(): return lax.ppermute(value, ('terms', 'rows'), pairs)  51.9 us
    pallas_call x1, Pallas kernels, orthogonal(): pl.pallas_call(kernel, out_shape=(shape((slab, width)),) + (shape(square,...  21.7 us
    pallas_call x2, Pallas kernels, apply_terms(): pl.pallas_call(kernel, out_shape=(shape((half, width)),) * 2, in_specs=[V...  4.15 us
  transfers between devices with their start and end apart: 56, of which 30 were waited for; matrix products, arithmetic and copies ran while one was open for 0% of the time, Pallas kernels for 15%

profile of v3, /device:TPU:8, one launch (start us, length us, event | category | flops | bytes accessed | tf_op | source)
XLA Modules:
  0.0 164.8 jit_solution(13141907407229024379)
XLA Ops:
  1.6 1.6 collective-permute-start
  7.0 1.7 %copy-done = f32[1,768,768]{2,1,0:T(8,128)S(1)} copy-done((f32[1,768,768]{2,1,0:T(8,128)S(1)}, f32[1,768,768]{2,1,0:T(8,128)}, u32[]{:S(2)}) %copy-start) | copy-done | bytes 2359320
  9.1 5.5 %collective-permute-done.refs_0_ = f32[48,768]{1,0:T(8,128)S(1)} collective-permute-done((f32[48,768]{1,0:T(8,128)S(1)}, f32[48,768]{1,0:T(8,128)S(1)}, u32[]{:S(2)}, u32[]{:S(2)}) %collective-permute-start) | collective-permute-done | bytes 147488 | tf_op jit(solution)/shard_map/ppermute | solution.py:64
  19.5 2.8 %collective-permute-done.5.refs_5_ = f32[72,768]{1,0:T(8,128)S(1)} collective-permute-done((f32[72,768]{1,0:T(8,128)S(1)}, f32[72,768]{1,0:T(8,128)S(1)}, u32[]{:S(2)}, u32[]{:S(2)}) %collective-permute-start.5) | collective-permute-done | bytes 221216 | tf_op jit(solution)/shard_map/ppermute | solution.py:64
  25.0 2.1 %apply.2 = (f32[96,768]{1,0:T(8,128)S(1)}, f32[96,768]{1,0:T(8,128)S(1)}) custom-call(f32[192,768]{1,0:T(8,128)S(1)} %get-tuple-element.58.refs_0_, f32[72,768]{1,0:T(8,128)S(1)} %get-tuple-element.59.refs_1_, f32[72,768]{1,0:T(8,128)S(1)} %collective-permute-done.3.refs_2_, f32[72,768]{1,0:T(8,128)S(1)} %get-tuple-element.60.refs_3_, ...), custom_call_target="tpu_custom_call" | custom-call | tf_op jit(solution)/shard_map/apply/pallas_call | solution.py:222
  33.8 2.4 %collective-permute-done.12.refs_3_ = f32[24,768]{1,0:T(8,128)S(1)} collective-permute-done((f32[24,768]{1,0:T(8,128)S(1)}, f32[24,768]{1,0:T(8,128)S(1)}, u32[]{:S(2)}, u32[]{:S(2)}) %collective-permute-start.12) | collective-permute-done | bytes 73760 | tf_op jit(solution)/shard_map/ppermute | solution.py:64
  36.9 4.3 %collective-permute-start.18 = (f32[24,768]{1,0:T(8,128)S(1)}, f32[24,768]{1,0:T(8,128)S(1)}, u32[]{:S(2)}, u32[]{:S(2)}) collective-permute-start(f32[24,768]{1,0:T(8,128)S(1)} %get-tuple-element.72.refs_0_), channel_id=1, source_target_pairs={{0,2},{1,3},{2,0},{3,1},{4,6},{5,7},{6,4},{7,5},{8,10},{9,11},{10,... | collective-permute-start | bytes 221192 | tf_op jit(solution)/shard_map/ppermute | solution.py:64
  43.3 1.8 %collective-permute-done.18.refs_1_ = f32[24,768]{1,0:T(8,128)S(1)} collective-permute-done((f32[24,768]{1,0:T(8,128)S(1)}, f32[24,768]{1,0:T(8,128)S(1)}, u32[]{:S(2)}, u32[]{:S(2)}) %collective-permute-start.18) | collective-permute-done | bytes 73760 | tf_op jit(solution)/shard_map/ppermute | solution.py:64
  50.7 6.1 %collective-permute-done.15.refs_3_ = f32[24,768]{1,0:T(8,128)S(1)} collective-permute-done((f32[24,768]{1,0:T(8,128)S(1)}, f32[24,768]{1,0:T(8,128)S(1)}, u32[]{:S(2)}, u32[]{:S(2)}) %collective-permute-start.15) | collective-permute-done | bytes 73760 | tf_op jit(solution)/shard_map/ppermute | solution.py:64
  62.4 2.1 %apply.3 = (f32[96,768]{1,0:T(8,128)S(1)}, f32[96,768]{1,0:T(8,128)S(1)}) custom-call(f32[96,768]{1,0:T(8,128)S(1)} %stack.4.refs_0_, f32[96,768]{1,0:T(8,128)S(1)} %collective-permute-done.16.refs_1_, f32[72,768]{1,0:T(8,128)S(1)} %stack.5.refs_2_, f32[72,768]{1,0:T(8,128)S(1)} %collective-permute-done.20.refs_3_, ...), custom_call_target="tpu_custom_call" | custom-call | tf_op jit(solution)/shard_map/apply/pallas_call | solution.py:222
  65.4 3.6 %collective-permute-done.47.refs_2_ = f32[48,768]{1,0:T(8,128)S(1)} collective-permute-done((f32[48,768]{1,0:T(8,128)S(1)}, f32[48,768]{1,0:T(8,128)S(1)}, u32[]{:S(2)}, u32[]{:S(2)}) %collective-permute-start.47) | collective-permute-done | bytes 147488 | tf_op jit(solution)/shard_map/ppermute | solution.py:64
  75.5 1.7 %collective-permute-done.30.refs_3_ = f32[24,768]{1,0:T(8,128)S(1)} collective-permute-done((f32[24,768]{1,0:T(8,128)S(1)}, f32[24,768]{1,0:T(8,128)S(1)}, u32[]{:S(2)}, u32[]{:S(2)}) %collective-permute-start.30) | collective-permute-done | bytes 73760 | tf_op jit(solution)/shard_map/ppermute | solution.py:64
  77.2 1.7 %collective-permute-start.35 = (f32[24,768]{1,0:T(8,128)S(1)}, f32[24,768]{1,0:T(8,128)S(1)}, u32[]{:S(2)}, u32[]{:S(2)}) collective-permute-start(f32[24,768]{1,0:T(8,128)S(1)} %step_piece.3.refs_0_), channel_id=1, source_target_pairs={{0,3},{1,2},{2,1},{3,0},{4,7},{5,6},{6,5},{7,4},{8,11},{9,10},{10,... | collective-permute-start | bytes 221192 | tf_op jit(solution)/shard_map/ppermute | solution.py:64
  81.0 1.6 collective-permute-start.52
  82.5 2.8 %collective-permute-start.36 = (f32[24,768]{1,0:T(8,128)S(1)}, f32[24,768]{1,0:T(8,128)S(1)}, u32[]{:S(2)}, u32[]{:S(2)}) collective-permute-start(f32[24,768]{1,0:T(8,128)S(1)} %step_piece.3.refs_0_), channel_id=1, source_target_pairs={{0,2},{1,3},{2,0},{3,1},{4,6},{5,7},{6,4},{7,5},{8,10},{9,11},{10,... | collective-permute-start | bytes 221192 | tf_op jit(solution)/shard_map/ppermute | solution.py:64
  85.7 2.1 %collective-permute-done.36.refs_1_ = f32[24,768]{1,0:T(8,128)S(1)} collective-permute-done((f32[24,768]{1,0:T(8,128)S(1)}, f32[24,768]{1,0:T(8,128)S(1)}, u32[]{:S(2)}, u32[]{:S(2)}) %collective-permute-start.36) | collective-permute-done | bytes 73760 | tf_op jit(solution)/shard_map/ppermute | solution.py:64
  87.8 1.9 %collective-permute-done.37.refs_2_ = f32[24,768]{1,0:T(8,128)S(1)} collective-permute-done((f32[24,768]{1,0:T(8,128)S(1)}, f32[24,768]{1,0:T(8,128)S(1)}, u32[]{:S(2)}, u32[]{:S(2)}) %collective-permute-start.37) | collective-permute-done | bytes 73760 | tf_op jit(solution)/shard_map/ppermute | solution.py:64
  93.9 5.3 %collective-permute-done.31.refs_1_ = f32[24,768]{1,0:T(8,128)S(1)} collective-permute-done((f32[24,768]{1,0:T(8,128)S(1)}, f32[24,768]{1,0:T(8,128)S(1)}, u32[]{:S(2)}, u32[]{:S(2)}) %collective-permute-start.31) | collective-permute-done | bytes 73760 | tf_op jit(solution)/shard_map/ppermute | solution.py:64
  102.1 6.4 %collective-permute-done.33.refs_3_ = f32[24,768]{1,0:T(8,128)S(1)} collective-permute-done((f32[24,768]{1,0:T(8,128)S(1)}, f32[24,768]{1,0:T(8,128)S(1)}, u32[]{:S(2)}, u32[]{:S(2)}) %collective-permute-start.33) | collective-permute-done | bytes 73760 | tf_op jit(solution)/shard_map/ppermute | solution.py:64
  109.7 1.6 collective-permute-start.54
  115.5 21.7 %orthogonal.1 = (f32[192,768]{1,0:T(8,128)}, bf16[768,768]{1,0:T(8,128)(2,1)S(1)}, bf16[768,768]{1,0:T(8,128)(2,1)S(1)}, bf16[192,768]{1,0:T(8,128)(2,1)S(1)}, bf16[192,768]{1,0:T(8,128)(2,1)S(1)}) custom-call(f32[96,768]{1,0:T(8,128)S(1)} %stack.6.refs_0_, f32[96,768]{1,0:T(8,128)S(1)} %collective-permute-done.34.refs_1_, f32[72,768]{1,0:T(8,128)S(1)} %stack.7.refs_2_, ...), custom_call_target="tpu_custom_call" | custom-call | tf_op jit(solution)/shard_map/orthogonal/pallas_call | solution.py:433
  137.3 13.0 %collective-permute-done.54.refs_2_ = f32[192,768]{1,0:T(8,128)S(1)} collective-permute-done((f32[192,768]{1,0:T(8,128)S(1)}, f32[192,768]{1,0:T(8,128)S(1)}, u32[]{:S(2)}, u32[]{:S(2)}) %collective-permute-start.54) | collective-permute-done | bytes 589856 | tf_op jit(solution)/shard_map/ppermute | solution.py:64
  150.3 11.4 %collective-permute-done.55.refs_3_ = f32[192,768]{1,0:T(8,128)S(1)} collective-permute-done((f32[192,768]{1,0:T(8,128)S(1)}, f32[192,768]{1,0:T(8,128)S(1)}, u32[]{:S(2)}, u32[]{:S(2)}) %collective-permute-start.55) | collective-permute-done | bytes 589856 | tf_op jit(solution)/shard_map/ppermute | solution.py:64
  161.6 3.2 %environment.1 = f32[192,768]{1,0:T(8,128)} custom-call(f32[192,768]{1,0:T(8,128)S(1)} %place_rows.1.refs_0_, f32[192,768]{1,0:T(8,128)S(1)} %collective-permute-done.53.refs_1_, f32[192,768]{1,0:T(8,128)S(1)} %collective-permute-done.54.refs_2_, f32[192,768]{1,0:T(8,128)S(1)} %collective-permute-done.55.refs_3_, ...), custom_call_target="tpu_custom_call" | custom-call | tf_op jit(solution)/shard_map/environment/pallas_call | solution.py:459
  (122 shorter events, 55.7 us)
Async XLA Ops:
  1.6 12.9 %collective-permute-start = (f32[48,768]{1,0:T(8,128)S(1)}, f32[48,768]{1,0:T(8,128)S(1)}, u32[]{:S(2)}, u32[]{:S(2)}) collective-permute-start(f32[48,768]{1,0:T(8,128)S(1)} %constant_dynamic-slice_fusion), channel_id=1, source_target_pairs={{0,3},{1,2},{2,1},{3,0},{4,7},{5,6},{6,5},{7,4},{8,11},{9,10},{10,... | collective-permute-start | bytes 442376 | tf_op jit(solution)/shard_map/ppermute | solution.py:64
  3.3 12.6 %collective-permute-start.1 = (f32[48,768]{1,0:T(8,128)S(1)}, f32[48,768]{1,0:T(8,128)S(1)}, u32[]{:S(2)}, u32[]{:S(2)}) collective-permute-start(f32[48,768]{1,0:T(8,128)S(1)} %constant_dynamic-slice_fusion), channel_id=1, source_target_pairs={{0,2},{1,3},{2,0},{3,1},{4,6},{5,7},{6,4},{7,5},{8,10},{9,11},{10,... | collective-permute-start | bytes 442376 | tf_op jit(solution)/shard_map/ppermute | solution.py:64
  4.4 11.5 %collective-permute-start.2 = (f32[48,768]{1,0:T(8,128)S(1)}, f32[48,768]{1,0:T(8,128)S(1)}, u32[]{:S(2)}, u32[]{:S(2)}) collective-permute-start(f32[48,768]{1,0:T(8,128)S(1)} %constant_dynamic-slice_fusion), channel_id=1, source_target_pairs={{0,1},{1,0},{2,3},{3,2},{4,5},{5,4},{6,7},{7,6},{8,9},{9,8},{10,11... | collective-permute-start | bytes 442376 | tf_op jit(solution)/shard_map/ppermute | solution.py:64
  32.3 24.6 %collective-permute-start.45 = (f32[96,768]{1,0:T(8,128)S(1)}, f32[96,768]{1,0:T(8,128)S(1)}, u32[]{:S(2)}, u32[]{:S(2)}) collective-permute-start(f32[96,768]{1,0:T(8,128)S(1)} %get-tuple-element.81), channel_id=1, source_target_pairs={{0,4},{1,5},{2,6},{3,7},{4,0},{5,1},{6,2},{7,3},{8,12},{9,13},{10,... | collective-permute-start | bytes 884744 | tf_op jit(solution)/shard_map/ppermute | solution.py:64
  36.9 8.2 %collective-permute-start.18 = (f32[24,768]{1,0:T(8,128)S(1)}, f32[24,768]{1,0:T(8,128)S(1)}, u32[]{:S(2)}, u32[]{:S(2)}) collective-permute-start(f32[24,768]{1,0:T(8,128)S(1)} %get-tuple-element.72.refs_0_), channel_id=1, source_target_pairs={{0,2},{1,3},{2,0},{3,1},{4,6},{5,7},{6,4},{7,5},{8,10},{9,11},{10,... | collective-permute-start | bytes 221192 | tf_op jit(solution)/shard_map/ppermute | solution.py:64
  45.6 11.8 %collective-permute-start.21 = (f32[72,768]{1,0:T(8,128)S(1)}, f32[72,768]{1,0:T(8,128)S(1)}, u32[]{:S(2)}, u32[]{:S(2)}) collective-permute-start(f32[72,768]{1,0:T(8,128)S(1)} %stack.5.refs_2_), channel_id=1, source_target_pairs={{0,8},{1,9},{2,10},{3,11},{4,12},{5,13},{6,14},{7,15},{8,0},{9,1},... | collective-permute-start | bytes 663560 | tf_op jit(solution)/shard_map/ppermute | solution.py:64
  47.1 11.0 %collective-permute-start.23 = (f32[72,768]{1,0:T(8,128)S(1)}, f32[72,768]{1,0:T(8,128)S(1)}, u32[]{:S(2)}, u32[]{:S(2)}) collective-permute-start(f32[72,768]{1,0:T(8,128)S(1)} %stack.5.refs_2_), channel_id=1, source_target_pairs={{0,16},{1,17},{2,18},{3,19},{4,20},{5,21},{6,22},{7,23},{8,24},{9,... | collective-permute-start | bytes 663560 | tf_op jit(solution)/shard_map/ppermute | solution.py:64
  47.7 10.3 %collective-permute-start.25 = (f32[72,768]{1,0:T(8,128)S(1)}, f32[72,768]{1,0:T(8,128)S(1)}, u32[]{:S(2)}, u32[]{:S(2)}) collective-permute-start(f32[72,768]{1,0:T(8,128)S(1)} %stack.5.refs_2_), channel_id=1, source_target_pairs={{0,24},{1,25},{2,26},{3,27},{4,28},{5,29},{6,30},{7,31},{8,16},{9,... | collective-permute-start | bytes 663560 | tf_op jit(solution)/shard_map/ppermute | solution.py:64
  49.1 7.6 %collective-permute-start.15 = (f32[24,768]{1,0:T(8,128)S(1)}, f32[24,768]{1,0:T(8,128)S(1)}, u32[]{:S(2)}, u32[]{:S(2)}) collective-permute-start(f32[24,768]{1,0:T(8,128)S(1)} %get-tuple-element.72.refs_0_), channel_id=1, source_target_pairs={{0,24},{1,25},{2,26},{3,27},{4,28},{5,29},{6,30},{7,31},{8,16},{9,... | collective-permute-start | bytes 221192 | tf_op jit(solution)/shard_map/ppermute | solution.py:64
  60.2 8.8 %collective-permute-start.47 = (f32[48,768]{1,0:T(8,128)S(1)}, f32[48,768]{1,0:T(8,128)S(1)}, u32[]{:S(2)}, u32[]{:S(2)}) collective-permute-start(f32[48,768]{1,0:T(8,128)S(1)} %get-tuple-element.84), channel_id=1, source_target_pairs={{0,16},{1,17},{2,18},{3,19},{4,20},{5,21},{6,22},{7,23},{8,24},{9,... | collective-permute-start | bytes 442376 | tf_op jit(solution)/shard_map/ppermute | solution.py:64
  69.8 9.1 %collective-permute-start.49 = (f32[96,768]{1,0:T(8,128)S(1)}, f32[96,768]{1,0:T(8,128)S(1)}, u32[]{:S(2)}, u32[]{:S(2)}) collective-permute-start(f32[96,768]{1,0:T(8,128)S(1)} %get-tuple-element.87), channel_id=1, source_target_pairs={{0,4},{1,5},{2,6},{3,7},{4,0},{5,1},{6,2},{7,3},{8,12},{9,13},{10,... | collective-permute-start | bytes 884744 | tf_op jit(solution)/shard_map/ppermute | solution.py:64
  77.2 8.0 %collective-permute-start.35 = (f32[24,768]{1,0:T(8,128)S(1)}, f32[24,768]{1,0:T(8,128)S(1)}, u32[]{:S(2)}, u32[]{:S(2)}) collective-permute-start(f32[24,768]{1,0:T(8,128)S(1)} %step_piece.3.refs_0_), channel_id=1, source_target_pairs={{0,3},{1,2},{2,1},{3,0},{4,7},{5,6},{6,5},{7,4},{8,11},{9,10},{10,... | collective-permute-start | bytes 221192 | tf_op jit(solution)/shard_map/ppermute | solution.py:64
  79.0 12.2 %collective-permute-start.50 = (f32[48,768]{1,0:T(8,128)S(1)}, f32[48,768]{1,0:T(8,128)S(1)}, u32[]{:S(2)}, u32[]{:S(2)}) collective-permute-start(f32[48,768]{1,0:T(8,128)S(1)} %get-tuple-element.89), channel_id=1, source_target_pairs={{0,8},{1,9},{2,10},{3,11},{4,12},{5,13},{6,14},{7,15},{8,0},{9,1},... | collective-permute-start | bytes 442376 | tf_op jit(solution)/shard_map/ppermute | solution.py:64
  80.2 11.7 %collective-permute-start.51 = (f32[48,768]{1,0:T(8,128)S(1)}, f32[48,768]{1,0:T(8,128)S(1)}, u32[]{:S(2)}, u32[]{:S(2)}) collective-permute-start(f32[48,768]{1,0:T(8,128)S(1)} %get-tuple-element.90), channel_id=1, source_target_pairs={{0,16},{1,17},{2,18},{3,19},{4,20},{5,21},{6,22},{7,23},{8,24},{9,... | collective-permute-start | bytes 442376 | tf_op jit(solution)/shard_map/ppermute | solution.py:64
  81.0 12.0 %collective-permute-start.52 = (f32[48,768]{1,0:T(8,128)S(1)}, f32[48,768]{1,0:T(8,128)S(1)}, u32[]{:S(2)}, u32[]{:S(2)}) collective-permute-start(f32[48,768]{1,0:T(8,128)S(1)} %get-tuple-element.91), channel_id=1, source_target_pairs={{0,24},{1,25},{2,26},{3,27},{4,28},{5,29},{6,30},{7,31},{8,16},{9,... | collective-permute-start | bytes 442376 | tf_op jit(solution)/shard_map/ppermute | solution.py:64
  89.7 20.0 %collective-permute-start.38 = (f32[72,768]{1,0:T(8,128)S(1)}, f32[72,768]{1,0:T(8,128)S(1)}, u32[]{:S(2)}, u32[]{:S(2)}) collective-permute-start(f32[72,768]{1,0:T(8,128)S(1)} %stack.7.refs_2_), channel_id=1, source_target_pairs={{0,4},{1,5},{2,6},{3,7},{4,0},{5,1},{6,2},{7,3},{8,12},{9,13},{10,... | collective-permute-start | bytes 663560 | tf_op jit(solution)/shard_map/ppermute | solution.py:64
  89.7 21.5 %collective-permute-start.39 = (f32[72,768]{1,0:T(8,128)S(1)}, f32[72,768]{1,0:T(8,128)S(1)}, u32[]{:S(2)}, u32[]{:S(2)}) collective-permute-start(f32[72,768]{1,0:T(8,128)S(1)} %stack.7.refs_2_), channel_id=1, source_target_pairs={{0,8},{1,9},{2,10},{3,11},{4,12},{5,13},{6,14},{7,15},{8,0},{9,1},... | collective-permute-start | bytes 663560 | tf_op jit(solution)/shard_map/ppermute | solution.py:64
  91.2 20.8 %collective-permute-start.41 = (f32[72,768]{1,0:T(8,128)S(1)}, f32[72,768]{1,0:T(8,128)S(1)}, u32[]{:S(2)}, u32[]{:S(2)}) collective-permute-start(f32[72,768]{1,0:T(8,128)S(1)} %stack.7.refs_2_), channel_id=1, source_target_pairs={{0,16},{1,17},{2,18},{3,19},{4,20},{5,21},{6,22},{7,23},{8,24},{9,... | collective-permute-start | bytes 663560 | tf_op jit(solution)/shard_map/ppermute | solution.py:64
  93.0 7.8 %collective-permute-start.32 = (f32[24,768]{1,0:T(8,128)S(1)}, f32[24,768]{1,0:T(8,128)S(1)}, u32[]{:S(2)}, u32[]{:S(2)}) collective-permute-start(f32[24,768]{1,0:T(8,128)S(1)} %step_piece.3.refs_0_), channel_id=1, source_target_pairs={{0,16},{1,17},{2,18},{3,19},{4,20},{5,21},{6,22},{7,23},{8,24},{9,... | collective-permute-start | bytes 221192 | tf_op jit(solution)/shard_map/ppermute | solution.py:64
  99.2 13.0 %collective-permute-start.43 = (f32[72,768]{1,0:T(8,128)S(1)}, f32[72,768]{1,0:T(8,128)S(1)}, u32[]{:S(2)}, u32[]{:S(2)}) collective-permute-start(f32[72,768]{1,0:T(8,128)S(1)} %stack.7.refs_2_), channel_id=1, source_target_pairs={{0,24},{1,25},{2,26},{3,27},{4,28},{5,29},{6,30},{7,31},{8,16},{9,... | collective-permute-start | bytes 663560 | tf_op jit(solution)/shard_map/ppermute | solution.py:64
  100.7 7.8 %collective-permute-start.33 = (f32[24,768]{1,0:T(8,128)S(1)}, f32[24,768]{1,0:T(8,128)S(1)}, u32[]{:S(2)}, u32[]{:S(2)}) collective-permute-start(f32[24,768]{1,0:T(8,128)S(1)} %step_piece.3.refs_0_), channel_id=1, source_target_pairs={{0,24},{1,25},{2,26},{3,27},{4,28},{5,29},{6,30},{7,31},{8,16},{9,... | collective-permute-start | bytes 221192 | tf_op jit(solution)/shard_map/ppermute | solution.py:64
  108.5 28.7 %collective-permute-start.53 = (f32[192,768]{1,0:T(8,128)S(1)}, f32[192,768]{1,0:T(8,128)S(1)}, u32[]{:S(2)}, u32[]{:S(2)}) collective-permute-start(f32[192,768]{1,0:T(8,128)S(1)} %place_rows.1.refs_0_), channel_id=1, source_target_pairs={{0,1},{1,0},{2,3},{3,2},{4,5},{5,4},{6,7},{7,6},{8,9},{9,8},{10,11... | collective-permute-start | bytes 1769480 | tf_op jit(solution)/shard_map/ppermute | solution.py:64
  109.7 40.6 %collective-permute-start.54 = (f32[192,768]{1,0:T(8,128)S(1)}, f32[192,768]{1,0:T(8,128)S(1)}, u32[]{:S(2)}, u32[]{:S(2)}) collective-permute-start(f32[192,768]{1,0:T(8,128)S(1)} %place_rows.1.refs_0_), channel_id=1, source_target_pairs={{0,2},{1,3},{2,0},{3,1},{4,6},{5,7},{6,4},{7,5},{8,10},{9,11},{10,... | collective-permute-start | bytes 1769480 | tf_op jit(solution)/shard_map/ppermute | solution.py:64
  111.3 50.4 %collective-permute-start.55 = (f32[192,768]{1,0:T(8,128)S(1)}, f32[192,768]{1,0:T(8,128)S(1)}, u32[]{:S(2)}, u32[]{:S(2)}) collective-permute-start(f32[192,768]{1,0:T(8,128)S(1)} %place_rows.1.refs_0_), channel_id=1, source_target_pairs={{0,3},{1,2},{2,1},{3,0},{4,7},{5,6},{6,5},{7,4},{8,11},{9,10},{10,... | collective-permute-start | bytes 1769480 | tf_op jit(solution)/shard_map/ppermute | solution.py:64
  (39 other events, 178.1 us)

commit v4 on v3

--- a/solution.py
+++ b/solution.py
@@ -129,7 +129,12 @@
 def exchange(places, own, away):
     received = places.swap(away, core=1)
     first, *others = pair_pieces(places, own, received)
-    return [first] + [places.swap(part, chip=slot + 1) for slot, part in enumerate(others)]
+    return [first] + to_chips(places, others)
+
+
+def to_chips(places, parts):
+    swapped = [places.swap(part, chip=slot) for slot, part in reversed(list(enumerate(parts, 1)))]
+    return swapped[::-1]
 
 
 def by_source(places, parts, whole, stride):
@@ -209,25 +214,39 @@
 def apply_terms(places, layout, parts, prepared):
     width = parts[0].shape[1]
     half = places.half
-
-    def kernel(*refs):
+    *left_halves, rh, rl = prepared
+
+    def first_kernel(*refs):
         count = len(parts)
-        lh_ref, ll_ref, rh_ref, rl_ref, keep_ref, send_ref, whole = refs[count:]
+        lh_ref, ll_ref, rh_ref, rl_ref, send_ref, mh_ref, ml_ref, whole = refs[count:]
         assemble(places, layout, refs[:count], put_in(whole))
         mapped = product((lh_ref[...], ll_ref[...]), halves(whole[...]))
-        total = product(halves(mapped), (rh_ref[...], rl_ref[...]))
-        keep_ref[...] = total[:half]
-        send_ref[...] = total[half:]
-
-    return pl.pallas_call(
-        kernel,
-        out_shape=(shape((half, width)),) * 2,
+        high, low = halves(mapped)
+        send_ref[...] = product((high[half:], low[half:]), (rh_ref[...], rl_ref[...]))
+        mh_ref[...], ml_ref[...] = high[:half], low[:half]
+
+    def second_kernel(mh_ref, ml_ref, rh_ref, rl_ref, keep_ref):
+        keep_ref[...] = product((mh_ref[...], ml_ref[...]), (rh_ref[...], rl_ref[...]))
+
+    send, high, low = pl.pallas_call(
+        first_kernel,
+        out_shape=(shape((half, width)),) + (shape((half, width), BF16),) * 2,
         in_specs=[VMEM] * (len(parts) + 4),
-        out_specs=(VMEM, VMEM),
+        out_specs=(VMEM,) * 3,
         scratch_shapes=[pltpu.VMEM((width, width), F32)],
         compiler_params=pltpu.CompilerParams(vmem_limit_bytes=10 * MIB),
         name="apply",
-    )(*parts, *prepared)
+    )(*parts, *left_halves, rh, rl)
+    received = places.swap(send, core=1)
+    keep = pl.pallas_call(
+        second_kernel,
+        out_shape=shape((half, width)),
+        in_specs=[VMEM] * 4,
+        out_specs=VMEM,
+        compiler_params=pltpu.CompilerParams(vmem_limit_bytes=4 * MIB),
+        name="apply_rest",
+    )(high, low, rh, rl)
+    return keep, received
 
 
 def add_pieces(places, keep, received):
@@ -296,7 +315,6 @@
 
 
 def spread(places, piece):
-    chips = range(1, places.chips)
     slots = list(reversed(range(1, places.rows)))
     layout, parts = [], []
 
@@ -307,9 +325,9 @@
         return [(row_slot, places.piece, place(chip_slot)) for chip_slot, row_slot in pairs]
 
     lines = [places.swap(piece, row=slot) for slot in slots]
-    own = [piece] + [places.swap(piece, chip=slot) for slot in chips]
+    own = [piece] + to_chips(places, [piece] * (places.chips - 1))
     mine = stack(lines)
-    gathered = [mine] + [places.swap(mine, chip=slot) for slot in chips]
+    gathered = [mine] + to_chips(places, [mine] * (places.chips - 1))
     own = stack(own)
     to_both_cores(places, layout, parts, blocks([(slot, 0) for slot in range(places.chips)]), own)
     for chip_slot, part in enumerate(gathered):
@@ -360,10 +378,9 @@
     )(*parts)
 
 
-def reduced(places, keep, send):
-    received = places.swap(send, core=1)
+def reduced(places, keep, received):
     own, *others = add_pieces(places, keep, received)
-    return [own] + [places.swap(part, chip=slot + 1) for slot, part in enumerate(others)]
+    return [own] + to_chips(places, others)
 
 
 def orthogonal(places, layout, parts):
@@ -441,13 +458,15 @@
     )(*parts)
 
 
-def environment(places, layout, parts, high, low, mine_high, mine_low):
+def environment(places, layout, parts, isometry, high, low, mine_high, mine_low):
     width = high.shape[0]
     slab = places.slab
 
     def kernel(*refs):
         count = len(parts)
-        high_ref, low_ref, mh_ref, ml_ref, out_ref, block_high, block_low = refs[count:]
+        iso_ref, high_ref, low_ref, mh_ref, ml_ref, iso_out, out_ref, block_high, block_low, sem = refs[count:]
+        out = pltpu.make_async_copy(iso_ref, iso_out, sem)
+        out.start()
 
         def store(start, height, value):
             block_high[pl.ds(start, height), :], block_low[pl.ds(start, height), :] = halves(value)
@@ -455,16 +474,17 @@
         assemble(places, layout, refs[:count], store)
         rotated = product((mh_ref[...], ml_ref[...]), (block_high[...], block_low[...]))
         out_ref[...] = product(halves(rotated), (high_ref[...], low_ref[...]))
-
-    return pl.pallas_call(
-        kernel,
-        out_shape=shape((slab, width)),
-        in_specs=[VMEM] * (len(parts) + 4),
-        out_specs=VMEM,
-        scratch_shapes=[pltpu.VMEM((width, width), BF16)] * 2,
+        out.wait()
+
+    return pl.pallas_call(
+        kernel,
+        out_shape=(shape((slab, width)),) * 2,
+        in_specs=[VMEM] * (len(parts) + 5),
+        out_specs=(pl.BlockSpec(memory_space=pl.ANY), VMEM),
+        scratch_shapes=[pltpu.VMEM((width, width), BF16)] * 2 + [pltpu.SemaphoreType.DMA],
         compiler_params=pltpu.CompilerParams(vmem_limit_bytes=10 * MIB),
         name="environment",
-    )(*parts, high, low, mine_high, mine_low)
+    )(*parts, isometry, high, low, mine_high, mine_low)
 
 
 def combine_pieces(pieces, source_list, list_count, weight_index, weight_table):
@@ -521,8 +541,7 @@
         *prepared, amplitudes, base = prepared
         layout, parts = [slabs[0]] + layout, [amplitudes] + parts
         for name in ("f", "x"):
-            keep, send = apply_terms(places, layout, parts, prepared)
-            pieces = reduced(places, keep, send)
+            pieces = reduced(places, *apply_terms(places, layout, parts, prepared))
             sent, *kept = step_piece(base, pieces, 2 if name == "f" else 1)
             layout, parts = spread(places, sent)
             base = kept[0] if kept else None
@@ -542,8 +561,7 @@
         combined = combined_slab(left, *lists)
         full = lax.all_gather(combined, "rows", axis=0, tiled=True)
         blocks = [lax.dynamic_slice_in_dim(full, (line ^ slot) * slab, slab, 0) for slot in every]
-    isometry, *turned = orthogonal(places, layout, parts)
-    new_environment = environment(places, slabs, blocks, *turned)
+    isometry, new_environment = environment(places, slabs, blocks, *orthogonal(places, layout, parts))
     return (isometry, new_environment[None])
 
 

time: 165 us -> 165 us (level)
  the two profiles are of different devices: /device:TPU:8 before, /device:TPU:0 now
where the time goes in v4:
time: 165 us; the launch traced here: 164 us
  waiting for transfers between devices  76.3 us (46%)
  starting transfers between devices  51.2 us (31%)
  Pallas kernels  31.3 us (19%)
  local copies, waits for them, and re-layouts  4.34 us (3%)
    ppermute x56, waiting for transfers between devices, swap(): return lax.ppermute(value, ('terms', 'rows'), pairs)  76.3 us
    ppermute x56, starting transfers between devices, swap(): return lax.ppermute(value, ('terms', 'rows'), pairs)  51.2 us
    pallas_call x1, Pallas kernels, orthogonal(): pl.pallas_call(kernel, out_shape=(shape((slab, width)),) + (shape(square,...  21 us
    pallas_call x2, Pallas kernels, apply_terms(): pl.pallas_call(first_kernel, out_shape=(shape((half, width)),) + (shape((...  4.27 us
    unnamed x14, local copies, waits for them, and re-layouts  3.42 us
  transfers between devices with their start and end apart: 56, of which 32 were waited for; matrix products, arithmetic and copies ran while one was open for 0% of the time, Pallas kernels for 16%

profile of v4, /device:TPU:0, one launch (start us, length us, event | category | flops | bytes accessed | tf_op | source)
XLA Modules:
  0.0 164.3 jit_solution(14868402678356529299)
XLA Ops:
  1.6 5.1 %collective-permute-start.11 = (f32[48,768]{1,0:T(8,128)S(1)}, f32[48,768]{1,0:T(8,128)S(1)}, u32[]{:S(2)}, u32[]{:S(2)}) collective-permute-start(f32[48,768]{1,0:T(8,128)S(1)} %constant_dynamic-slice_fusion), channel_id=1, source_target_pairs={{0,3},{1,2},{2,1},{3,0},{4,7},{5,6},{6,5},{7,4},{8,11},{9,10},{10,... | collective-permute-start | bytes 442376 | tf_op jit(solution)/shard_map/ppermute | solution.py:64
  7.4 1.7 %copy-done = f32[1,768,768]{2,1,0:T(8,128)S(1)} copy-done((f32[1,768,768]{2,1,0:T(8,128)S(1)}, f32[1,768,768]{2,1,0:T(8,128)}, u32[]{:S(2)}) %copy-start) | copy-done | bytes 2359320
  11.5 7.7 %collective-permute-done.12.refs_1_ = f32[48,768]{1,0:T(8,128)S(1)} collective-permute-done((f32[48,768]{1,0:T(8,128)S(1)}, f32[48,768]{1,0:T(8,128)S(1)}, u32[]{:S(2)}, u32[]{:S(2)}) %collective-permute-start.12) | collective-permute-done | bytes 147488 | tf_op jit(solution)/shard_map/ppermute | solution.py:64
  22.8 3.0 %collective-permute-done.16.refs_5_ = f32[72,768]{1,0:T(8,128)S(1)} collective-permute-done((f32[72,768]{1,0:T(8,128)S(1)}, f32[72,768]{1,0:T(8,128)S(1)}, u32[]{:S(2)}, u32[]{:S(2)}) %collective-permute-start.16) | collective-permute-done | bytes 221216 | tf_op jit(solution)/shard_map/ppermute | solution.py:64
  28.5 2.1 %apply.2 = (f32[96,768]{1,0:T(8,128)S(1)}, bf16[96,768]{1,0:T(8,128)(2,1)S(1)}, bf16[96,768]{1,0:T(8,128)(2,1)S(1)}) custom-call(f32[192,768]{1,0:T(8,128)S(1)} %get-tuple-element.74.refs_0_, f32[72,768]{1,0:T(8,128)S(1)} %get-tuple-element.75.refs_1_, f32[72,768]{1,0:T(8,128)S(1)} %collective-permute-done.14.refs_2_, ...), custom_call_target="tpu_custom_call" | custom-call | tf_op jit(solution)/shard_map/apply/pallas_call | solution.py:231
  37.3 2.4 %collective-permute-done.23.refs_3_ = f32[24,768]{1,0:T(8,128)S(1)} collective-permute-done((f32[24,768]{1,0:T(8,128)S(1)}, f32[24,768]{1,0:T(8,128)S(1)}, u32[]{:S(2)}, u32[]{:S(2)}) %collective-permute-start.23) | collective-permute-done | bytes 73760 | tf_op jit(solution)/shard_map/ppermute | solution.py:64
  39.8 2.4 %collective-permute-start.28 = (f32[24,768]{1,0:T(8,128)S(1)}, f32[24,768]{1,0:T(8,128)S(1)}, u32[]{:S(2)}, u32[]{:S(2)}) collective-permute-start(f32[24,768]{1,0:T(8,128)S(1)} %get-tuple-element.89.refs_0_), channel_id=1, source_target_pairs={{0,3},{1,2},{2,1},{3,0},{4,7},{5,6},{6,5},{7,4},{8,11},{9,10},{10,... | collective-permute-start | bytes 221192 | tf_op jit(solution)/shard_map/ppermute | solution.py:64
  42.2 2.1 %collective-permute-start.30 = (f32[24,768]{1,0:T(8,128)S(1)}, f32[24,768]{1,0:T(8,128)S(1)}, u32[]{:S(2)}, u32[]{:S(2)}) collective-permute-start(f32[24,768]{1,0:T(8,128)S(1)} %get-tuple-element.89.refs_0_), channel_id=1, source_target_pairs={{0,1},{1,0},{2,3},{3,2},{4,5},{5,4},{6,7},{7,6},{8,9},{9,8},{10,11... | collective-permute-start | bytes 221192 | tf_op jit(solution)/shard_map/ppermute | solution.py:64
  50.3 1.6 collective-permute-start.36
  51.9 1.6 collective-permute-done.25.refs_2_
  53.5 6.3 %collective-permute-done.26.refs_3_ = f32[24,768]{1,0:T(8,128)S(1)} collective-permute-done((f32[24,768]{1,0:T(8,128)S(1)}, f32[24,768]{1,0:T(8,128)S(1)}, u32[]{:S(2)}, u32[]{:S(2)}) %collective-permute-start.26) | collective-permute-done | bytes 73760 | tf_op jit(solution)/shard_map/ppermute | solution.py:64
  65.8 2.1 %apply.3 = (f32[96,768]{1,0:T(8,128)S(1)}, bf16[96,768]{1,0:T(8,128)(2,1)S(1)}, bf16[96,768]{1,0:T(8,128)(2,1)S(1)}) custom-call(f32[96,768]{1,0:T(8,128)S(1)} %stack.4.refs_0_, f32[96,768]{1,0:T(8,128)S(1)} %collective-permute-done.27.refs_1_, f32[72,768]{1,0:T(8,128)S(1)} %stack.5.refs_2_, f32[72,768]{1,0:T(8,128)S(1)} %collective-permute-done.31.refs_3_, ...), custom_call_target="tpu_custom_call" | custom-call | tf_op jit(solution)/shard_map/apply/pallas_call | solution.py:231
  69.0 3.0 %collective-permute-done.2.refs_2_ = f32[48,768]{1,0:T(8,128)S(1)} collective-permute-done((f32[48,768]{1,0:T(8,128)S(1)}, f32[48,768]{1,0:T(8,128)S(1)}, u32[]{:S(2)}, u32[]{:S(2)}) %collective-permute-start.2) | collective-permute-done | bytes 147488 | tf_op jit(solution)/shard_map/ppermute | solution.py:64
  79.1 1.8 %collective-permute-done.41.refs_3_ = f32[24,768]{1,0:T(8,128)S(1)} collective-permute-done((f32[24,768]{1,0:T(8,128)S(1)}, f32[24,768]{1,0:T(8,128)S(1)}, u32[]{:S(2)}, u32[]{:S(2)}) %collective-permute-start.41) | collective-permute-done | bytes 73760 | tf_op jit(solution)/shard_map/ppermute | solution.py:64
  80.8 2.2 %collective-permute-start.46 = (f32[24,768]{1,0:T(8,128)S(1)}, f32[24,768]{1,0:T(8,128)S(1)}, u32[]{:S(2)}, u32[]{:S(2)}) collective-permute-start(f32[24,768]{1,0:T(8,128)S(1)} %step_piece.3.refs_0_), channel_id=1, source_target_pairs={{0,3},{1,2},{2,1},{3,0},{4,7},{5,6},{6,5},{7,4},{8,11},{9,10},{10,... | collective-permute-start | bytes 221192 | tf_op jit(solution)/shard_map/ppermute | solution.py:64
  87.2 1.7 %collective-permute-start.48 = (f32[24,768]{1,0:T(8,128)S(1)}, f32[24,768]{1,0:T(8,128)S(1)}, u32[]{:S(2)}, u32[]{:S(2)}) collective-permute-start(f32[24,768]{1,0:T(8,128)S(1)} %step_piece.3.refs_0_), channel_id=1, source_target_pairs={{0,1},{1,0},{2,3},{3,2},{4,5},{5,4},{6,7},{7,6},{8,9},{9,8},{10,11... | collective-permute-start | bytes 221192 | tf_op jit(solution)/shard_map/ppermute | solution.py:64
  88.9 3.1 %collective-permute-done.47.refs_1_ = f32[24,768]{1,0:T(8,128)S(1)} collective-permute-done((f32[24,768]{1,0:T(8,128)S(1)}, f32[24,768]{1,0:T(8,128)S(1)}, u32[]{:S(2)}, u32[]{:S(2)}) %collective-permute-start.47) | collective-permute-done | bytes 73760 | tf_op jit(solution)/shard_map/ppermute | solution.py:64
  98.0 4.9 %collective-permute-done.42.refs_1_ = f32[24,768]{1,0:T(8,128)S(1)} collective-permute-done((f32[24,768]{1,0:T(8,128)S(1)}, f32[24,768]{1,0:T(8,128)S(1)}, u32[]{:S(2)}, u32[]{:S(2)}) %collective-permute-start.42) | collective-permute-done | bytes 73760 | tf_op jit(solution)/shard_map/ppermute | solution.py:64
  105.2 4.0 %collective-permute-done.44.refs_3_ = f32[24,768]{1,0:T(8,128)S(1)} collective-permute-done((f32[24,768]{1,0:T(8,128)S(1)}, f32[24,768]{1,0:T(8,128)S(1)}, u32[]{:S(2)}, u32[]{:S(2)}) %collective-permute-start.44) | collective-permute-done | bytes 73760 | tf_op jit(solution)/shard_map/ppermute | solution.py:64
  109.2 2.0 %collective-permute-start.10 = (f32[192,768]{1,0:T(8,128)S(1)}, f32[192,768]{1,0:T(8,128)S(1)}, u32[]{:S(2)}, u32[]{:S(2)}) collective-permute-start(f32[192,768]{1,0:T(8,128)S(1)} %place_rows.1.refs_0_), channel_id=1, source_target_pairs={{0,3},{1,2},{2,1},{3,0},{4,7},{5,6},{6,5},{7,4},{8,11},{9,10},{10,... | collective-permute-start | bytes 1769480 | tf_op jit(solution)/shard_map/ppermute | solution.py:64
  111.2 2.4 %collective-permute-start.9 = (f32[192,768]{1,0:T(8,128)S(1)}, f32[192,768]{1,0:T(8,128)S(1)}, u32[]{:S(2)}, u32[]{:S(2)}) collective-permute-start(f32[192,768]{1,0:T(8,128)S(1)} %place_rows.1.refs_0_), channel_id=1, source_target_pairs={{0,2},{1,3},{2,0},{3,1},{4,6},{5,7},{6,4},{7,5},{8,10},{9,11},{10,... | collective-permute-start | bytes 1769480 | tf_op jit(solution)/shard_map/ppermute | solution.py:64
  117.1 21.0 %orthogonal.1 = (f32[192,768]{1,0:T(8,128)S(1)}, bf16[768,768]{1,0:T(8,128)(2,1)S(1)}, bf16[768,768]{1,0:T(8,128)(2,1)S(1)}, bf16[192,768]{1,0:T(8,128)(2,1)S(1)}, bf16[192,768]{1,0:T(8,128)(2,1)S(1)}) custom-call(f32[96,768]{1,0:T(8,128)S(1)} %stack.6.refs_0_, f32[96,768]{1,0:T(8,128)S(1)} %collective-permute-done.45.refs_1_, f32[72,768]{1,0:T(8,128)S(1)} %stack.7.refs_2_, ...), custom_call_target="tpu_custom_call" | custom-call | tf_op jit(solution)/shard_map/orthogonal/pallas_call | solution.py:450
  138.7 22.2 %collective-permute-done.9.refs_2_ = f32[192,768]{1,0:T(8,128)S(1)} collective-permute-done((f32[192,768]{1,0:T(8,128)S(1)}, f32[192,768]{1,0:T(8,128)S(1)}, u32[]{:S(2)}, u32[]{:S(2)}) %collective-permute-start.9) | collective-permute-done | bytes 589856 | tf_op jit(solution)/shard_map/ppermute | solution.py:64
  160.9 3.2 %environment.1 = (f32[192,768]{1,0:T(8,128)}, f32[192,768]{1,0:T(8,128)}) custom-call(f32[192,768]{1,0:T(8,128)S(1)} %place_rows.1.refs_0_, f32[192,768]{1,0:T(8,128)S(1)} %collective-permute-done.8.refs_1_, f32[192,768]{1,0:T(8,128)S(1)} %collective-permute-done.9.refs_2_, f32[192,768]{1,0:T(8,128)S(1)} %collective-permute-done.10.refs_3_, ...), custom_call_target="tpu_custom_call" | custom-call | tf_op jit(solution)/shard_map/environment/pallas_call | solution.py:479
  (124 shorter events, 53.6 us)
Async XLA Ops:
  1.6 9.9 %collective-permute-start.11 = (f32[48,768]{1,0:T(8,128)S(1)}, f32[48,768]{1,0:T(8,128)S(1)}, u32[]{:S(2)}, u32[]{:S(2)}) collective-permute-start(f32[48,768]{1,0:T(8,128)S(1)} %constant_dynamic-slice_fusion), channel_id=1, source_target_pairs={{0,3},{1,2},{2,1},{3,0},{4,7},{5,6},{6,5},{7,4},{8,11},{9,10},{10,... | collective-permute-start | bytes 442376 | tf_op jit(solution)/shard_map/ppermute | solution.py:64
  6.7 12.5 %collective-permute-start.12 = (f32[48,768]{1,0:T(8,128)S(1)}, f32[48,768]{1,0:T(8,128)S(1)}, u32[]{:S(2)}, u32[]{:S(2)}) collective-permute-start(f32[48,768]{1,0:T(8,128)S(1)} %constant_dynamic-slice_fusion), channel_id=1, source_target_pairs={{0,2},{1,3},{2,0},{3,1},{4,6},{5,7},{6,4},{7,5},{8,10},{9,11},{10,... | collective-permute-start | bytes 442376 | tf_op jit(solution)/shard_map/ppermute | solution.py:64
  6.7 12.5 %collective-permute-start.13 = (f32[48,768]{1,0:T(8,128)S(1)}, f32[48,768]{1,0:T(8,128)S(1)}, u32[]{:S(2)}, u32[]{:S(2)}) collective-permute-start(f32[48,768]{1,0:T(8,128)S(1)} %constant_dynamic-slice_fusion), channel_id=1, source_target_pairs={{0,1},{1,0},{2,3},{3,2},{4,5},{5,4},{6,7},{7,6},{8,9},{9,8},{10,11... | collective-permute-start | bytes 442376 | tf_op jit(solution)/shard_map/ppermute | solution.py:64
  35.9 24.0 %collective-permute-start = (f32[96,768]{1,0:T(8,128)S(1)}, f32[96,768]{1,0:T(8,128)S(1)}, u32[]{:S(2)}, u32[]{:S(2)}) collective-permute-start(f32[96,768]{1,0:T(8,128)S(1)} %get-tuple-element.54), channel_id=1, source_target_pairs={{0,4},{1,5},{2,6},{3,7},{4,0},{5,1},{6,2},{7,3},{8,12},{9,13},{10,... | collective-permute-start | bytes 884744 | tf_op jit(solution)/shard_map/ppermute | solution.py:64
  39.8 6.9 %collective-permute-start.28 = (f32[24,768]{1,0:T(8,128)S(1)}, f32[24,768]{1,0:T(8,128)S(1)}, u32[]{:S(2)}, u32[]{:S(2)}) collective-permute-start(f32[24,768]{1,0:T(8,128)S(1)} %get-tuple-element.89.refs_0_), channel_id=1, source_target_pairs={{0,3},{1,2},{2,1},{3,0},{4,7},{5,6},{6,5},{7,4},{8,11},{9,10},{10,... | collective-permute-start | bytes 221192 | tf_op jit(solution)/shard_map/ppermute | solution.py:64
  46.7 6.8 %collective-permute-start.25 = (f32[24,768]{1,0:T(8,128)S(1)}, f32[24,768]{1,0:T(8,128)S(1)}, u32[]{:S(2)}, u32[]{:S(2)}) collective-permute-start(f32[24,768]{1,0:T(8,128)S(1)} %get-tuple-element.89.refs_0_), channel_id=1, source_target_pairs={{0,16},{1,17},{2,18},{3,19},{4,20},{5,21},{6,22},{7,23},{8,24},{9,... | collective-permute-start | bytes 221192 | tf_op jit(solution)/shard_map/ppermute | solution.py:64
  48.3 12.1 %collective-permute-start.32 = (f32[72,768]{1,0:T(8,128)S(1)}, f32[72,768]{1,0:T(8,128)S(1)}, u32[]{:S(2)}, u32[]{:S(2)}) collective-permute-start(f32[72,768]{1,0:T(8,128)S(1)} %stack.5.refs_2_), channel_id=1, source_target_pairs={{0,8},{1,9},{2,10},{3,11},{4,12},{5,13},{6,14},{7,15},{8,0},{9,1},... | collective-permute-start | bytes 663560 | tf_op jit(solution)/shard_map/ppermute | solution.py:64
  49.7 11.9 %collective-permute-start.34 = (f32[72,768]{1,0:T(8,128)S(1)}, f32[72,768]{1,0:T(8,128)S(1)}, u32[]{:S(2)}, u32[]{:S(2)}) collective-permute-start(f32[72,768]{1,0:T(8,128)S(1)} %stack.5.refs_2_), channel_id=1, source_target_pairs={{0,16},{1,17},{2,18},{3,19},{4,20},{5,21},{6,22},{7,23},{8,24},{9,... | collective-permute-start | bytes 663560 | tf_op jit(solution)/shard_map/ppermute | solution.py:64
  50.3 11.3 %collective-permute-start.36 = (f32[72,768]{1,0:T(8,128)S(1)}, f32[72,768]{1,0:T(8,128)S(1)}, u32[]{:S(2)}, u32[]{:S(2)}) collective-permute-start(f32[72,768]{1,0:T(8,128)S(1)} %stack.5.refs_2_), channel_id=1, source_target_pairs={{0,24},{1,25},{2,26},{3,27},{4,28},{5,29},{6,30},{7,31},{8,16},{9,... | collective-permute-start | bytes 663560 | tf_op jit(solution)/shard_map/ppermute | solution.py:64
  62.2 6.8 %collective-permute-start.1 = (f32[48,768]{1,0:T(8,128)S(1)}, f32[48,768]{1,0:T(8,128)S(1)}, u32[]{:S(2)}, u32[]{:S(2)}) collective-permute-start(f32[48,768]{1,0:T(8,128)S(1)} %get-tuple-element.56), channel_id=1, source_target_pairs={{0,8},{1,9},{2,10},{3,11},{4,12},{5,13},{6,14},{7,15},{8,0},{9,1},... | collective-permute-start | bytes 442376 | tf_op jit(solution)/shard_map/ppermute | solution.py:64
  63.2 8.8 %collective-permute-start.2 = (f32[48,768]{1,0:T(8,128)S(1)}, f32[48,768]{1,0:T(8,128)S(1)}, u32[]{:S(2)}, u32[]{:S(2)}) collective-permute-start(f32[48,768]{1,0:T(8,128)S(1)} %get-tuple-element.57), channel_id=1, source_target_pairs={{0,16},{1,17},{2,18},{3,19},{4,20},{5,21},{6,22},{7,23},{8,24},{9,... | collective-permute-start | bytes 442376 | tf_op jit(solution)/shard_map/ppermute | solution.py:64
  64.6 7.4 %collective-permute-start.3 = (f32[48,768]{1,0:T(8,128)S(1)}, f32[48,768]{1,0:T(8,128)S(1)}, u32[]{:S(2)}, u32[]{:S(2)}) collective-permute-start(f32[48,768]{1,0:T(8,128)S(1)} %get-tuple-element.58), channel_id=1, source_target_pairs={{0,24},{1,25},{2,26},{3,27},{4,28},{5,29},{6,30},{7,31},{8,16},{9,... | collective-permute-start | bytes 442376 | tf_op jit(solution)/shard_map/ppermute | solution.py:64
  72.8 10.2 %collective-permute-start.4 = (f32[96,768]{1,0:T(8,128)S(1)}, f32[96,768]{1,0:T(8,128)S(1)}, u32[]{:S(2)}, u32[]{:S(2)}) collective-permute-start(f32[96,768]{1,0:T(8,128)S(1)} %get-tuple-element.60), channel_id=1, source_target_pairs={{0,4},{1,5},{2,6},{3,7},{4,0},{5,1},{6,2},{7,3},{8,12},{9,13},{10,... | collective-permute-start | bytes 884744 | tf_op jit(solution)/shard_map/ppermute | solution.py:64
  83.1 11.5 %collective-permute-start.5 = (f32[48,768]{1,0:T(8,128)S(1)}, f32[48,768]{1,0:T(8,128)S(1)}, u32[]{:S(2)}, u32[]{:S(2)}) collective-permute-start(f32[48,768]{1,0:T(8,128)S(1)} %get-tuple-element.62), channel_id=1, source_target_pairs={{0,8},{1,9},{2,10},{3,11},{4,12},{5,13},{6,14},{7,15},{8,0},{9,1},... | collective-permute-start | bytes 442376 | tf_op jit(solution)/shard_map/ppermute | solution.py:64
  84.5 11.5 %collective-permute-start.6 = (f32[48,768]{1,0:T(8,128)S(1)}, f32[48,768]{1,0:T(8,128)S(1)}, u32[]{:S(2)}, u32[]{:S(2)}) collective-permute-start(f32[48,768]{1,0:T(8,128)S(1)} %get-tuple-element.63), channel_id=1, source_target_pairs={{0,16},{1,17},{2,18},{3,19},{4,20},{5,21},{6,22},{7,23},{8,24},{9,... | collective-permute-start | bytes 442376 | tf_op jit(solution)/shard_map/ppermute | solution.py:64
  85.2 12.2 %collective-permute-start.7 = (f32[48,768]{1,0:T(8,128)S(1)}, f32[48,768]{1,0:T(8,128)S(1)}, u32[]{:S(2)}, u32[]{:S(2)}) collective-permute-start(f32[48,768]{1,0:T(8,128)S(1)} %get-tuple-element.64), channel_id=1, source_target_pairs={{0,24},{1,25},{2,26},{3,27},{4,28},{5,29},{6,30},{7,31},{8,16},{9,... | collective-permute-start | bytes 442376 | tf_op jit(solution)/shard_map/ppermute | solution.py:64
  92.4 18.8 %collective-permute-start.50 = (f32[72,768]{1,0:T(8,128)S(1)}, f32[72,768]{1,0:T(8,128)S(1)}, u32[]{:S(2)}, u32[]{:S(2)}) collective-permute-start(f32[72,768]{1,0:T(8,128)S(1)} %stack.7.refs_2_), channel_id=1, source_target_pairs={{0,8},{1,9},{2,10},{3,11},{4,12},{5,13},{6,14},{7,15},{8,0},{9,1},... | collective-permute-start | bytes 663560 | tf_op jit(solution)/shard_map/ppermute | solution.py:64
  93.9 17.3 %collective-permute-start.52 = (f32[72,768]{1,0:T(8,128)S(1)}, f32[72,768]{1,0:T(8,128)S(1)}, u32[]{:S(2)}, u32[]{:S(2)}) collective-permute-start(f32[72,768]{1,0:T(8,128)S(1)} %stack.7.refs_2_), channel_id=1, source_target_pairs={{0,16},{1,17},{2,18},{3,19},{4,20},{5,21},{6,22},{7,23},{8,24},{9,... | collective-permute-start | bytes 663560 | tf_op jit(solution)/shard_map/ppermute | solution.py:64
  94.5 19.1 %collective-permute-start.54 = (f32[72,768]{1,0:T(8,128)S(1)}, f32[72,768]{1,0:T(8,128)S(1)}, u32[]{:S(2)}, u32[]{:S(2)}) collective-permute-start(f32[72,768]{1,0:T(8,128)S(1)} %stack.7.refs_2_), channel_id=1, source_target_pairs={{0,24},{1,25},{2,26},{3,27},{4,28},{5,29},{6,30},{7,31},{8,16},{9,... | collective-permute-start | bytes 663560 | tf_op jit(solution)/shard_map/ppermute | solution.py:64
  95.9 7.0 %collective-permute-start.42 = (f32[24,768]{1,0:T(8,128)S(1)}, f32[24,768]{1,0:T(8,128)S(1)}, u32[]{:S(2)}, u32[]{:S(2)}) collective-permute-start(f32[24,768]{1,0:T(8,128)S(1)} %step_piece.3.refs_0_), channel_id=1, source_target_pairs={{0,8},{1,9},{2,10},{3,11},{4,12},{5,13},{6,14},{7,15},{8,0},{9,1},... | collective-permute-start | bytes 221192 | tf_op jit(solution)/shard_map/ppermute | solution.py:64
  103.0 10.7 %collective-permute-start.49 = (f32[72,768]{1,0:T(8,128)S(1)}, f32[72,768]{1,0:T(8,128)S(1)}, u32[]{:S(2)}, u32[]{:S(2)}) collective-permute-start(f32[72,768]{1,0:T(8,128)S(1)} %stack.7.refs_2_), channel_id=1, source_target_pairs={{0,4},{1,5},{2,6},{3,7},{4,0},{5,1},{6,2},{7,3},{8,12},{9,13},{10,... | collective-permute-start | bytes 663560 | tf_op jit(solution)/shard_map/ppermute | solution.py:64
  109.2 28.9 %collective-permute-start.10 = (f32[192,768]{1,0:T(8,128)S(1)}, f32[192,768]{1,0:T(8,128)S(1)}, u32[]{:S(2)}, u32[]{:S(2)}) collective-permute-start(f32[192,768]{1,0:T(8,128)S(1)} %place_rows.1.refs_0_), channel_id=1, source_target_pairs={{0,3},{1,2},{2,1},{3,0},{4,7},{5,6},{6,5},{7,4},{8,11},{9,10},{10,... | collective-permute-start | bytes 1769480 | tf_op jit(solution)/shard_map/ppermute | solution.py:64
  111.2 27.5 %collective-permute-start.8 = (f32[192,768]{1,0:T(8,128)S(1)}, f32[192,768]{1,0:T(8,128)S(1)}, u32[]{:S(2)}, u32[]{:S(2)}) collective-permute-start(f32[192,768]{1,0:T(8,128)S(1)} %place_rows.1.refs_0_), channel_id=1, source_target_pairs={{0,1},{1,0},{2,3},{3,2},{4,5},{5,4},{6,7},{7,6},{8,9},{9,8},{10,11... | collective-permute-start | bytes 1769480 | tf_op jit(solution)/shard_map/ppermute | solution.py:64
  111.2 49.7 %collective-permute-start.9 = (f32[192,768]{1,0:T(8,128)S(1)}, f32[192,768]{1,0:T(8,128)S(1)}, u32[]{:S(2)}, u32[]{:S(2)}) collective-permute-start(f32[192,768]{1,0:T(8,128)S(1)} %place_rows.1.refs_0_), channel_id=1, source_target_pairs={{0,2},{1,3},{2,0},{3,1},{4,6},{5,7},{6,4},{7,5},{8,10},{9,11},{10,... | collective-permute-start | bytes 1769480 | tf_op jit(solution)/shard_map/ppermute | solution.py:64
  (39 other events, 172.3 us)
